TPU v7x, 32 devices: a whole 2x2x4 slice. The times are simulated.
32 devices in a mesh: rows: 2 (over y), dp: 16 (over z, x, core).
Axes of the slice: x: 2, y: 2, z: 4, core: 2. Of those that a mesh axis runs over, the one named last changes fastest.
Arguments:
- images: bfloat16 [48, 14, 14, 512], P('dp', 'rows'), may hold values from -6 to 6
- cotangent: bfloat16 [48, 14, 14, 512], P('dp', 'rows'), may hold values from -6 to 6
- attn_in_weight: bfloat16 [2, 512, 1536], P(None, 'dp'), may hold values from -0.25 to 0.25
- attn_out_weight: bfloat16 [2, 512, 512], P(None, 'dp'), may hold values from -0.75 to 0.75
- mlp_in_weight: bfloat16 [2, 512, 2048], P(None, 'dp'), may hold values from -0.25 to 0.25
- mlp_out_weight: bfloat16 [2, 2048, 512], P(None, 'dp'), may hold values from -0.125 to 0.125
- norm1_gain: bfloat16 [2, 512], P(None, 'dp'), may hold values from 0.5 to 1.5
- norm1_bias: bfloat16 [2, 512], P(None, 'dp'), may hold values from -1.5 to 1.5
- attn_in_bias: bfloat16 [2, 1024], P(None, 'dp'), may hold values from -1.5 to 1.5
- attn_out_bias: bfloat16 [2, 512], P(None, 'dp'), may hold values from -1.5 to 1.5
- norm2_gain: bfloat16 [2, 512], P(None, 'dp'), may hold values from 0.5 to 1.5
- norm2_bias: bfloat16 [2, 512], P(None, 'dp'), may hold values from -1.5 to 1.5
- mlp_in_bias: bfloat16 [2, 2048], P(None, 'dp'), may hold values from -1.5 to 1.5
- mlp_out_bias: bfloat16 [2, 512], P(None, 'dp'), may hold values from -1.5 to 1.5
- bias_table: float32 [2, 169, 16], replicated, may hold values from -5 to 303
- region_labels: int32 [14, 14], replicated, may hold values from 0 to 2
- table_index: int32 [49, 49], replicated, may hold values from 0 to 168
Outputs:
- final_out: bfloat16 [48, 14, 14, 512], P('dp', 'rows')
- input_grad: float32 [48, 14, 14, 512], P('dp', 'rows')
- grad_attn_in_weight: float32 [2, 512, 1536], P(None, 'dp')
- grad_attn_out_weight: float32 [2, 512, 512], P(None, 'dp')
- grad_mlp_in_weight: float32 [2, 512, 2048], P(None, 'dp')
- grad_mlp_out_weight: float32 [2, 2048, 512], P(None, 'dp')
- grad_norm1_gain: float32 [2, 512], P(None, 'dp')
- grad_norm1_bias: float32 [2, 512], P(None, 'dp')
- grad_attn_in_bias: float32 [2, 1024], P(None, 'dp')
- grad_attn_out_bias: float32 [2, 512], P(None, 'dp')
- grad_norm2_gain: float32 [2, 512], P(None, 'dp')
- grad_norm2_bias: float32 [2, 512], P(None, 'dp')
- grad_mlp_in_bias: float32 [2, 2048], P(None, 'dp')
- grad_mlp_out_bias: float32 [2, 512], P(None, 'dp')
- grad_bias_table: float32 [2, 169, 16], replicated
All inputs are finite; a program needn't handle non-finite values.
Results may differ from a plain program's by a relative error of at most 0.015.
Values may be sent and summed in bfloat16 or wider, within the bound.
A program may use at most 192 MiB of HBM per device.

v0:
```python
import jax
import jax.numpy as jnp
from jax import lax
from jax.sharding import PartitionSpec as P

C = 512
HEADS = 16
HEAD_DIM = 32
WIN = 7
GRID = 14
SHIFT = 3
LAYERS = 2
REL = 169


EPS = 1e-05
NEG = -1e30
SQRT_HALF = 0.7071067811865476
INV_ROOT_TAU = 0.3989422804014327


def swapped(array, axis, distance):
    return lax.ppermute(array, axis, [(i, i ^ 1 << distance) for i in range(lax.axis_size(axis))])


def product(spec, left, right):
    return jnp.einsum(spec, left, right, preferred_element_type=jnp.float32)


def outer(left, right):
    left_flat = left.reshape(-1, left.shape[-1])
    right_flat = right.reshape(-1, right.shape[-1])
    return lax.dot_general(
        left_flat, right_flat, (((0,), (0,)), ((), ())), preferred_element_type=jnp.float32
    )


def back_product(grad_rows, weight):
    return lax.dot_general(
        grad_rows,
        weight,
        (((grad_rows.ndim - 1,), (1,)), ((), ())),
        preferred_element_type=jnp.float32,
    )


def token_total(values):
    return jnp.sum(values.reshape(-1, values.shape[-1]), axis=0)


def to_windows(grid):
    num_images, grid_rows, grid_cols, channels = grid.shape
    split = grid.reshape(num_images, grid_rows // WIN, WIN, grid_cols // WIN, WIN, channels)
    return split.transpose(0, 1, 3, 2, 4, 5).reshape(
        num_images, grid_rows // WIN * (grid_cols // WIN), WIN * WIN, channels
    )


def from_windows(window_rows, grid_rows, grid_cols):
    num_images = window_rows.shape[0]
    channels = window_rows.shape[-1]
    split = window_rows.reshape(num_images, grid_rows // WIN, grid_cols // WIN, WIN, WIN, channels)
    return split.transpose(0, 1, 3, 2, 4, 5).reshape(num_images, grid_rows, grid_cols, channels)


def layernorm_apply(values, gain_vector, offset_vector):
    average = jnp.mean(values, axis=-1, keepdims=True)
    centered_input = values - average
    variance = jnp.mean(centered_input * centered_input, axis=-1, keepdims=True)
    inverse_deviation = lax.rsqrt(variance + EPS)
    standardized = centered_input * inverse_deviation
    return (standardized * gain_vector + offset_vector, standardized, inverse_deviation)


def layernorm_reverse(output_gradient, standardized, inverse_deviation, gain_vector):
    standardized_gradient = output_gradient * gain_vector
    input_gradient_rows = inverse_deviation * (
        standardized_gradient
        - jnp.mean(standardized_gradient, axis=-1, keepdims=True)
        - standardized * jnp.mean(standardized_gradient * standardized, axis=-1, keepdims=True)
    )
    return (
        input_gradient_rows,
        token_total(output_gradient * standardized),
        token_total(output_gradient),
    )


def gelu_value(preactivation):
    return preactivation * 0.5 * (1.0 + lax.erf(preactivation * SQRT_HALF))


def gelu_slope(preactivation):
    return (
        0.5 * (1.0 + lax.erf(preactivation * SQRT_HALF))
        + preactivation * jnp.exp(-0.5 * preactivation * preactivation) * INV_ROOT_TAU
    )


def split_heads(rows):
    return rows.reshape(rows.shape[:-1] + (HEADS, HEAD_DIM))


def masked_scores(window_queries, window_keys, pos_bias, allowed):
    scores = (
        product("bwqhd,bwkhd->bwhqk", split_heads(window_queries), split_heads(window_keys))
        + pos_bias[None, None]
    )
    return jnp.where(allowed[None, :, None], scores, NEG)


def attend(window_queries, window_keys, window_values, pos_bias, allowed):
    scores = masked_scores(window_queries, window_keys, pos_bias, allowed)
    row_max = jnp.max(scores, axis=-1, keepdims=True)
    log_partition = row_max + jnp.log(jnp.sum(jnp.exp(scores - row_max), axis=-1, keepdims=True))
    attn_probs = jnp.exp(scores - log_partition).astype(jnp.bfloat16)
    context = product("bwhqk,bwkhd->bwqhd", attn_probs, split_heads(window_values))
    return (context.reshape(window_queries.shape).astype(jnp.bfloat16), log_partition)


def attend_back(
    window_queries, window_keys, window_values, pos_bias, allowed, log_partition, grad_context
):
    scores = masked_scores(window_queries, window_keys, pos_bias, allowed)
    attn_probs = jnp.exp(scores - log_partition)
    grad_heads = split_heads(grad_context)
    grad_probs = product("bwqhd,bwkhd->bwhqk", grad_heads, split_heads(window_values))
    grad_values = product("bwhqk,bwqhd->bwkhd", attn_probs.astype(jnp.bfloat16), grad_heads)
    grad_scores = attn_probs * (
        grad_probs - jnp.sum(attn_probs * grad_probs, axis=-1, keepdims=True)
    )
    table_term = jnp.sum(grad_scores, axis=(0, 1))
    scores_bf = grad_scores.astype(jnp.bfloat16)
    grad_query = product("bwhqk,bwkhd->bwqhd", scores_bf, split_heads(window_keys))
    grad_keys = product("bwhqk,bwqhd->bwkhd", scores_bf, split_heads(window_queries))
    shape = window_queries.shape
    return (
        grad_query.reshape(shape),
        grad_keys.reshape(shape),
        grad_values.reshape(shape),
        table_term,
    )


def lookup(table_part, table_index):
    picked = jnp.take(table_part, table_index.reshape(-1), axis=0)
    return picked.T.reshape(HEADS, WIN * WIN, WIN * WIN)


def enter_grid(normalized_tokens, shifted):
    if not shifted:
        return to_windows(normalized_tokens)
    incoming = swapped(normalized_tokens[:, :SHIFT], "rows", 0)
    grid = jnp.concatenate([normalized_tokens[:, SHIFT:], incoming], axis=1)
    return to_windows(jnp.roll(grid, -SHIFT, axis=2))


def leave_grid(context, shifted):
    grid = from_windows(context, WIN, GRID)
    if not shifted:
        return grid
    grid = jnp.roll(grid, SHIFT, axis=2)
    incoming = swapped(grid[:, WIN - SHIFT :], "rows", 0)
    return jnp.concatenate([incoming, grid[:, : WIN - SHIFT]], axis=1)


def enter_grad(grad_context, shifted):
    if not shifted:
        return to_windows(grad_context)
    incoming = swapped(grad_context[:, :SHIFT], "rows", 0)
    grid = jnp.concatenate([grad_context[:, SHIFT:], incoming], axis=1)
    return to_windows(jnp.roll(grid, -SHIFT, axis=2))


def leave_grad(grad_window, shifted):
    grid = from_windows(grad_window, WIN, GRID)
    if not shifted:
        return grid
    grid = jnp.roll(grid, SHIFT, axis=2)
    incoming = swapped(grid[:, WIN - SHIFT :].astype(jnp.bfloat16), "rows", 0).astype(jnp.float32)
    return jnp.concatenate([incoming, grid[:, : WIN - SHIFT]], axis=1)


def layer_forward(residual_tokens, params, table_part, table_index, allowed, shifted):
    (
        in_weight,
        out_weight,
        up_weight,
        down_weight,
        first_gain,
        first_offset,
        in_bias,
        out_bias,
        second_gain,
        second_offset,
        up_bias,
        down_bias,
    ) = params
    normalized_tokens, first_standardized, first_scale = layernorm_apply(
        residual_tokens, first_gain, first_offset
    )
    window_input = enter_grid(normalized_tokens.astype(jnp.bfloat16), shifted)
    packed = jnp.dot(window_input, in_weight, preferred_element_type=jnp.float32)
    window_queries = ((packed[..., :C] + in_bias[:C]) * HEAD_DIM ** (-0.5)).astype(jnp.bfloat16)
    window_keys = packed[..., C : 2 * C].astype(jnp.bfloat16)
    window_values = (packed[..., 2 * C :] + in_bias[C:]).astype(jnp.bfloat16)
    pos_bias = lookup(table_part, table_index)
    context, log_partition = attend(window_queries, window_keys, window_values, pos_bias, allowed)
    local_context = leave_grid(context, shifted)
    attended_residual = (
        residual_tokens
        + jnp.dot(local_context, out_weight, preferred_element_type=jnp.float32)
        + out_bias
    )
    second_normalized, second_standardized, second_scale = layernorm_apply(
        attended_residual, second_gain, second_offset
    )
    hidden_units = second_normalized.astype(jnp.bfloat16)
    preactivation = jnp.dot(hidden_units, up_weight, preferred_element_type=jnp.float32) + up_bias
    activated_units = gelu_value(preactivation).astype(jnp.bfloat16)
    result = (
        attended_residual
        + jnp.dot(activated_units, down_weight, preferred_element_type=jnp.float32)
        + down_bias
    )
    retained_state = (
        first_standardized,
        first_scale,
        window_input,
        window_queries,
        window_keys,
        window_values,
        log_partition,
        local_context,
        second_standardized,
        second_scale,
        hidden_units,
        preactivation,
        activated_units,
    )
    return (result, retained_state)


def layer_backward(
    grad_flow, params, table_part, table_index, allowed, onehot, shifted, retained_state
):
    (
        in_weight,
        out_weight,
        up_weight,
        down_weight,
        first_gain,
        first_offset,
        in_bias,
        out_bias,
        second_gain,
        second_offset,
        up_bias,
        down_bias,
    ) = params
    (
        first_standardized,
        first_scale,
        window_input,
        window_queries,
        window_keys,
        window_values,
        log_partition,
        local_context,
        second_standardized,
        second_scale,
        hidden_units,
        preactivation,
        activated_units,
    ) = retained_state
    grad_bf = grad_flow.astype(jnp.bfloat16)
    grad_down = outer(activated_units, grad_bf)
    grad_down_bias = token_total(grad_flow)
    grad_active = back_product(grad_bf, down_weight)
    grad_pre = grad_active * gelu_slope(preactivation)
    grad_pre_bf = grad_pre.astype(jnp.bfloat16)
    grad_upw = outer(hidden_units, grad_pre_bf)
    grad_up_bias = token_total(grad_pre)
    hidden_gradient = back_product(grad_pre_bf, up_weight)
    attention_share, second_gain_gradient, second_offset_gradient = layernorm_reverse(
        hidden_gradient, second_standardized, second_scale, second_gain
    )
    grad_mixed = grad_flow + attention_share
    mixed_bf = grad_mixed.astype(jnp.bfloat16)
    grad_outw = outer(local_context, mixed_bf)
    grad_out_bias = token_total(grad_mixed)
    grad_context = back_product(mixed_bf, out_weight).astype(jnp.bfloat16)
    grad_context_win = enter_grad(grad_context, shifted)
    pos_bias = lookup(table_part, table_index)
    grad_query, grad_keys, grad_values, table_term = attend_back(
        window_queries,
        window_keys,
        window_values,
        pos_bias,
        allowed,
        log_partition,
        grad_context_win,
    )
    grad_query = grad_query * HEAD_DIM ** (-0.5)
    grad_packed = jnp.concatenate([grad_query, grad_keys, grad_values], axis=-1).astype(
        jnp.bfloat16
    )
    grad_inw = outer(window_input, grad_packed)
    grad_in_bias = jnp.concatenate([token_total(grad_query), token_total(grad_values)])
    normalized_gradient = leave_grad(back_product(grad_packed, in_weight), shifted)
    residual_share, first_gain_gradient, first_offset_gradient = layernorm_reverse(
        normalized_gradient, first_standardized, first_scale, first_gain
    )
    grad_stream = grad_mixed + residual_share
    grad_table = lax.dot_general(
        onehot,
        table_term.reshape(HEADS, -1),
        (((0,), (1,)), ((), ())),
        precision=lax.Precision.HIGHEST,
    )
    grads = (
        grad_inw,
        grad_outw,
        grad_upw,
        grad_down,
        first_gain_gradient,
        first_offset_gradient,
        grad_in_bias,
        grad_out_bias,
        second_gain_gradient,
        second_offset_gradient,
        grad_up_bias,
        grad_down_bias,
    )
    return (grad_stream, grads, grad_table)


def as_params(gathered):
    return tuple(
        (
            member if position < 4 else member.astype(jnp.float32)
            for position, member in enumerate(gathered)
        )
    )


def fetch_layer(pieces):
    return (
        lax.all_gather(pieces[0], "dp", axis=0, tiled=True),
        lax.all_gather(pieces[1], "dp", axis=0, tiled=True),
        lax.all_gather(pieces[2], "dp", axis=0, tiled=True),
        lax.all_gather(pieces[3], "dp", axis=0, tiled=True),
        lax.all_gather(pieces[4], "dp", axis=0, tiled=True),
        lax.all_gather(pieces[5], "dp", axis=0, tiled=True),
        lax.all_gather(pieces[6], "dp", axis=0, tiled=True),
        lax.all_gather(pieces[7], "dp", axis=0, tiled=True),
        lax.all_gather(pieces[8], "dp", axis=0, tiled=True),
        lax.all_gather(pieces[9], "dp", axis=0, tiled=True),
        lax.all_gather(pieces[10], "dp", axis=0, tiled=True),
        lax.all_gather(pieces[11], "dp", axis=0, tiled=True),
    )


def reduce_grads(grads):
    shards = (
        lax.psum_scatter(grads[0], "dp", scatter_dimension=0, tiled=True),
        lax.psum_scatter(grads[1], "dp", scatter_dimension=0, tiled=True),
        lax.psum_scatter(grads[2], "dp", scatter_dimension=0, tiled=True),
        lax.psum_scatter(grads[3], "dp", scatter_dimension=0, tiled=True),
        lax.psum_scatter(grads[4], "dp", scatter_dimension=0, tiled=True),
        lax.psum_scatter(grads[5], "dp", scatter_dimension=0, tiled=True),
        lax.psum_scatter(grads[6], "dp", scatter_dimension=0, tiled=True),
        lax.psum_scatter(grads[7], "dp", scatter_dimension=0, tiled=True),
        lax.psum_scatter(grads[8], "dp", scatter_dimension=0, tiled=True),
        lax.psum_scatter(grads[9], "dp", scatter_dimension=0, tiled=True),
        lax.psum_scatter(grads[10], "dp", scatter_dimension=0, tiled=True),
        lax.psum_scatter(grads[11], "dp", scatter_dimension=0, tiled=True),
    )
    return (
        lax.psum(shards[0].astype(jnp.bfloat16), "rows").astype(jnp.float32),
        lax.psum(shards[1].astype(jnp.bfloat16), "rows").astype(jnp.float32),
        lax.psum(shards[2].astype(jnp.bfloat16), "rows").astype(jnp.float32),
        lax.psum(shards[3].astype(jnp.bfloat16), "rows").astype(jnp.float32),
        lax.psum(shards[4].astype(jnp.bfloat16), "rows").astype(jnp.float32),
        lax.psum(shards[5].astype(jnp.bfloat16), "rows").astype(jnp.float32),
        lax.psum(shards[6].astype(jnp.bfloat16), "rows").astype(jnp.float32),
        lax.psum(shards[7].astype(jnp.bfloat16), "rows").astype(jnp.float32),
        lax.psum(shards[8].astype(jnp.bfloat16), "rows").astype(jnp.float32),
        lax.psum(shards[9].astype(jnp.bfloat16), "rows").astype(jnp.float32),
        lax.psum(shards[10].astype(jnp.bfloat16), "rows").astype(jnp.float32),
        lax.psum(shards[11].astype(jnp.bfloat16), "rows").astype(jnp.float32),
    )


def per_device(
    images,
    cotangent,
    attn_in_weight,
    attn_out_weight,
    mlp_in_weight,
    mlp_out_weight,
    norm1_gain,
    norm1_bias,
    attn_in_bias,
    attn_out_bias,
    norm2_gain,
    norm2_bias,
    mlp_in_bias,
    mlp_out_bias,
    bias_table,
    region_labels,
    table_index,
):
    sharded = (
        attn_in_weight,
        attn_out_weight,
        mlp_in_weight,
        mlp_out_weight,
        norm1_gain,
        norm1_bias,
        attn_in_bias,
        attn_out_bias,
        norm2_gain,
        norm2_bias,
        mlp_in_bias,
        mlp_out_bias,
    )
    half_index = lax.axis_index("rows")
    local_labels = lax.dynamic_slice_in_dim(region_labels, half_index * WIN, WIN, 0)
    label_tiles = to_windows(local_labels[None, :, :, None])[0, :, :, 0]
    shifted_allowed = label_tiles[:, :, None] == label_tiles[:, None, :]
    allowed_pair = (jnp.ones_like(shifted_allowed), shifted_allowed)
    onehot = (table_index.reshape(-1)[:, None] == jnp.arange(REL, dtype=jnp.int32)[None, :]).astype(
        jnp.float32
    )
    residual_tokens = images.astype(jnp.float32)
    kept_params = []
    saved_all = []
    for layer_no in range(LAYERS):
        params = as_params(fetch_layer(tuple((member[layer_no] for member in sharded))))
        kept_params.append(params)
        residual_tokens, retained_state = layer_forward(
            residual_tokens,
            params,
            bias_table[layer_no],
            table_index,
            allowed_pair[layer_no % 2],
            layer_no % 2 == 1,
        )
        saved_all.append(retained_state)
    final_out = residual_tokens.astype(jnp.bfloat16)
    grad_flow = cotangent.astype(jnp.float32)
    reduced_all = [None] * LAYERS
    tables_all = [None] * LAYERS
    for layer_no in reversed(range(LAYERS)):
        params = kept_params[layer_no]
        grad_flow, grads, tables_all[layer_no] = layer_backward(
            grad_flow,
            params,
            bias_table[layer_no],
            table_index,
            allowed_pair[layer_no % 2],
            onehot,
            layer_no % 2 == 1,
            saved_all[layer_no],
        )
        reduced_all[layer_no] = reduce_grads(grads)
    table_total = lax.psum(jnp.stack(tables_all), ("rows", "dp"))
    stacked = tuple(
        (
            jnp.stack([reduced_all[layer_no][position] for layer_no in range(LAYERS)])
            for position in range(12)
        )
    )
    return (
        final_out,
        grad_flow,
        stacked[0],
        stacked[1],
        stacked[2],
        stacked[3],
        stacked[4],
        stacked[5],
        stacked[6],
        stacked[7],
        stacked[8],
        stacked[9],
        stacked[10],
        stacked[11],
        table_total,
    )


def solution(mesh):
    return jax.shard_map(
        per_device,
        mesh=mesh,
        in_specs=(
            P("dp", "rows", None, None),
            P("dp", "rows", None, None),
            P(None, "dp", None),
            P(None, "dp", None),
            P(None, "dp", None),
            P(None, "dp", None),
            P(None, "dp"),
            P(None, "dp"),
            P(None, "dp"),
            P(None, "dp"),
            P(None, "dp"),
            P(None, "dp"),
            P(None, "dp"),
            P(None, "dp"),
            P(),
            P(),
            P(),
        ),
        out_specs=(
            P("dp", "rows", None, None),
            P("dp", "rows", None, None),
            P(None, "dp", None),
            P(None, "dp", None),
            P(None, "dp", None),
            P(None, "dp", None),
            P(None, "dp"),
            P(None, "dp"),
            P(None, "dp"),
            P(None, "dp"),
            P(None, "dp"),
            P(None, "dp"),
            P(None, "dp"),
            P(None, "dp"),
            P(),
        ),
        check_vma=False,
    )
```

profile of v0, /device:TPU:0, one launch (start us, length us, event | category | flops | bytes accessed | tf_op | source)
XLA Modules:
  0.0 998.8 jit_solution(10137238297828627652)
XLA Ops:
  28.7 63.5 %all-reduce.31 = (bf16[512]{0:T(512)(128)(2,1)S(1)}, bf16[512]{0:T(512)(128)(2,1)S(1)}, bf16[1024]{0:T(1024)(128)(2,1)S(1)}, bf16[512]{0:T(512)(128)(2,1)S(1)}, ...) all-reduce(bf16[512]{0:T(512)(128)(2,1)S(1)} %dynamic-update-slice., ...), channel_id=3, replica_groups=mesh['rows'=2,'dp'=16] {'dp'}, use_global_device_ids=true, to_apply=%add.1 | all-reduce | flops 8192 | bytes 32768
  98.7 17.1 %all-gather.21 = bf16[1,2048]{1,0:T(2,128)(2,1)S(1)} all-gather(bf16[1,128]{1,0:T(2,128)(2,1)S(1)} %get-tuple-element.122), channel_id=23, replica_groups=mesh['rows'=2,'dp'=16] {'dp'}, dimensions={1}, use_global_device_ids=true | all-gather | bytes 4352 | tf_op jit(solution)/shard_map/all_gather | solution.py:359
  116.5 19.2 %all-gather.9 = bf16[1,2048]{1,0:T(2,128)(2,1)S(1)} all-gather(bf16[1,128]{1,0:T(2,128)(2,1)S(1)} %get-tuple-element.123), channel_id=11, replica_groups=mesh['rows'=2,'dp'=16] {'dp'}, dimensions={1}, use_global_device_ids=true | all-gather | bytes 4352 | tf_op jit(solution)/shard_map/all_gather | solution.py:359
  138.3 20.1 %all-gather.4 = bf16[1,512,512]{2,1,0:T(8,128)(2,1)S(1)} all-gather(bf16[1,32,512]{2,1,0:T(8,128)(2,1)S(1)} %get-tuple-element.111), channel_id=6, replica_groups=mesh['rows'=2,'dp'=16] {'dp'}, dimensions={1}, use_global_device_ids=true | all-gather | bytes 557056 | tf_op jit(solution)/shard_map/all_gather | solution.py:350
  158.4 4.2 gather_fusion
  162.7 5.6 gather_fusion.1
  168.3 3.4 select_bitcast_fusion
  182.4 2.4 add_reduce_fusion
  191.9 4.6 multiply_convert_fusion.1
  196.6 3.0 fusion.170
  201.0 5.3 collective-permute-done
  213.7 2.4 fusion.10
  219.3 2.9 copy.257
  222.3 3.2 convert_element_type.289
  228.9 23.5 %all-gather.16 = bf16[1,512,512]{2,1,0:T(8,128)(2,1)} all-gather(bf16[1,32,512]{2,1,0:T(8,128)(2,1)S(1)} %copy-done.72), channel_id=18, replica_groups=mesh['rows'=2,'dp'=16] {'dp'}, dimensions={1}, use_global_device_ids=true | all-gather | bytes 557056 | tf_op jit(solution)/shard_map/all_gather | solution.py:350
  261.7 5.0 multiply_convert_fusion
  266.8 4.9 fusion.173
  277.0 2.4 convolution_bitcast_fusion.4
  285.6 3.2 reshape_reshape.18
  288.9 2.9 copy.263
  291.8 2.7 multiply_reduce_fusion.1
  294.5 2.3 bitcast_convert_fusion.1
  312.2 3.2 concatenate.70
  317.2 2.9 mul.370
  324.0 2.4 fusion.174
  334.1 2.8 reshape_reshape.19
  336.9 3.1 copy.280
  340.0 4.1 multiply_reduce_fusion
  346.7 3.8 fusion.152
  357.5 2.4 fusion.172
  363.0 59.0 %all-reduce.30 = (bf16[512]{0:T(512)(128)(2,1)}, bf16[512]{0:T(512)(128)(2,1)}, bf16[512]{0:T(512)(128)(2,1)}, bf16[512]{0:T(512)(128)(2,1)}, bf16[1024]{0:T(102...) all-reduce(f32[512]{0:T(512)S(1)} %copy-done.92, ...), channel_id=35, replica_groups=mesh['rows'=2,'dp'=16] {'dp'}, use_global_device_ids=true, to_apply=%region_42.44.clone | all-reduce | flops 12288 | bytes 73728
  425.9 2.6 fusion.175
  437.9 44.8 %reduce-scatter.13.cloned.1.call-done = f32[32,512]{1,0:T(8,128)} async-done(((f32[512,512]{1,0:T(8,128)}), f32[32,512]{1,0:T(8,128)}) %reduce-scatter.13.cloned.1.call-update) | async-done | bytes 65552 | tf_op jit(solution)/shard_map/reduce_scatter | solution.py:367
  484.2 4.0 fusion.60
  494.0 2.7 fusion.54
  498.2 3.3 convolution_bitcast_fusion
  503.1 3.4 convolution_bitcast_fusion.2
  508.1 3.5 convolution_bitcast_fusion.3
  513.2 3.2 convolution_bitcast_fusion.1
  517.8 3.4 fusion.49
  524.6 42.1 %psum.199 = f32[2,169,16]{1,2,0:T(8,128)} all-reduce(f32[2,169,16]{1,2,0:T(8,128)S(1)} %pad_maximum_fusion.6), channel_id=1, replica_groups=mesh['rows'=2,'dp'=16] {'rows','dp'}, use_global_device_ids=true, to_apply=%region_91.93 | all-reduce | flops 5408 | bytes 43264 | tf_op jit(solution)/shard_map/psum | solution.py:468
  570.5 9.5 reduce-scatter.11.cloned.1.call-done
  581.6 67.5 %reduce-scatter.9.cloned.1.call-done = f32[32,1536]{1,0:T(8,128)} async-done(((f32[512,1536]{1,0:T(8,128)}), f32[32,1536]{1,0:T(8,128)}) %reduce-scatter.9.cloned.1.call-update) | async-done | bytes 196624 | tf_op jit(solution)/shard_map/reduce_scatter | solution.py:366
  650.7 73.8 %reduce-scatter.23.cloned.1.call-done = f32[128,512]{1,0:T(8,128)} async-done(((f32[2048,512]{1,0:T(8,128)}), f32[128,512]{1,0:T(8,128)}) %reduce-scatter.23.cloned.1.call-update) | async-done | bytes 262160 | tf_op jit(solution)/shard_map/reduce_scatter | solution.py:369
  726.2 74.1 %reduce-scatter.19.cloned.1.call-done = f32[32,2048]{1,0:T(8,128)} async-done(((f32[512,2048]{1,0:T(8,128)}), f32[32,2048]{1,0:T(8,128)}) %reduce-scatter.19.cloned.1.call-update) | async-done | bytes 262160 | tf_op jit(solution)/shard_map/reduce_scatter | solution.py:368
  801.9 73.9 %reduce-scatter.17.cloned.1.call-done = f32[32,2048]{1,0:T(8,128)} async-done(((f32[512,2048]{1,0:T(8,128)}), f32[32,2048]{1,0:T(8,128)}) %reduce-scatter.17.cloned.1.call-update) | async-done | bytes 262160 | tf_op jit(solution)/shard_map/reduce_scatter | solution.py:368
  877.3 73.9 %reduce-scatter.21.cloned.1.call-done = f32[128,512]{1,0:T(8,128)} async-done(((f32[2048,512]{1,0:T(8,128)}), f32[128,512]{1,0:T(8,128)}) %reduce-scatter.21.cloned.1.call-update) | async-done | bytes 262160 | tf_op jit(solution)/shard_map/reduce_scatter | solution.py:369
  957.0 29.4 %all-reduce.39.cloned.1.call-done = (bf16[1,32,1536]{2,1,0:T(8,128)(2,1)}, bf16[1,32,1536]{2,1,0:T(8,128)(2,1)}, bf16[1,32,2048]{2,1,0:T(8,128)(2,1)}, bf16[1,32...) async-done(((bf16[1,32,1536]{2,1,0:T(8,128)(2,1)}, bf16[1,32,1536]{2,1,0:T(8,128)(2,1)}, bf16[1,32,2048]{2,1,0:T(8,128)(2,1)}, ...) | async-done | bytes 720912 | tf_op jit(solution)/shard_map/psum | solution.py:380
  (599 shorter events, 176.5 us)
Async XLA Ops:
  7.2 90.2 %copy-start = (s32[14,14]{1,0:T(8,128)S(1)}, s32[14,14]{1,0:T(8,128)}, u32[]{:S(2)}) copy-start(s32[14,14]{1,0:T(8,128)} %param.34) | copy-start | bytes 2356
  7.2 129.1 %copy-start.9 = (bf16[3,7,14,512]{3,2,1,0:T(8,128)(2,1)S(1)}, bf16[3,7,14,512]{3,2,1,0:T(8,128)(2,1)}, u32[]{:S(2)}) copy-start(bf16[3,7,14,512]{3,2,1,0:T(8,128)(2,1)} %param.19) | copy-start | bytes 903172
  7.2 129.6 %copy-start.85 = (f32[2,169,16]{1,2,0:T(8,128)S(1)}, f32[2,169,16]{1,2,0:T(8,128)}, u32[]{:S(2)}) copy-start(f32[2,169,16]{1,2,0:T(8,128)} %param.33) | copy-start | bytes 64900
  7.2 129.6 %copy-start.79 = (bf16[2,32,512]{2,1,0:T(8,128)(2,1)S(1)}, bf16[2,32,512]{2,1,0:T(8,128)(2,1)}, u32[]{:S(2)}) copy-start(bf16[2,32,512]{2,1,0:T(8,128)(2,1)} %param.22) | copy-start | bytes 196612
  7.2 168.8 %all-gather.31.cloned.1.call-start = ((), (), s32[]{:S(2)}) async-start(), calls=%async_computation.16 | async-start | bytes 1671168 | tf_op jit(solution)/shard_map/all_gather | solution.py:349
  9.0 182.9 %all-gather.33.cloned.1.call-start = ((), (), s32[]{:S(2)}) async-start(), calls=%async_computation.17 | async-start | bytes 2228224 | tf_op jit(solution)/shard_map/all_gather | solution.py:351
  10.7 185.8 %all-gather.35.cloned.1.call-start = ((), (), s32[]{:S(2)}) async-start(), calls=%async_computation.18 | async-start | bytes 2228224 | tf_op jit(solution)/shard_map/all_gather | solution.py:352
  12.5 195.1 %all-gather.37.cloned.1.call-start = ((), (), s32[]{:S(2)}) async-start(), calls=%async_computation.19 | async-start | bytes 1671168 | tf_op jit(solution)/shard_map/all_gather | solution.py:349
  13.1 248.6 %all-gather.39.cloned.1.call-start = ((), (), s32[]{:S(2)}) async-start(), calls=%async_computation.20 | async-start | bytes 2228224 | tf_op jit(solution)/shard_map/all_gather | solution.py:351
  13.7 253.1 %all-gather.41.cloned.1.call-start = ((), (), s32[]{:S(2)}) async-start(), calls=%async_computation.21 | async-start | bytes 2228224 | tf_op jit(solution)/shard_map/all_gather | solution.py:352
  14.2 422.2 %reduce-scatter.15.cloned.1.call-start = ((), (), s32[]{:S(2)}) async-start(), calls=%async_computation.11 | async-start | bytes 1114112 | tf_op jit(solution)/shard_map/reduce_scatter | solution.py:367
  15.2 122.2 %copy-start.77 = (s32[2401]{0:T(1024)}, s32[2401]{0:T(1024)S(1)}, u32[]{:S(2)}) copy-start(s32[2401]{0:T(1024)S(1)} %reshape.354) | copy-start | bytes 28816
  136.4 26.2 %copy-start.66 = (f32[3,7,14]{2,1,0:T(8,128)}, f32[3,7,14]{2,1,0:T(8,128)S(1)}, u32[]{:S(2)}) copy-start(f32[3,7,14]{2,1,0:T(8,128)S(1)} %broadcast_multiply_fusion.11) | copy-start | bytes 3532
  136.7 26.0 %copy-start.70 = (f32[3,7,14]{2,1,0:T(8,128)}, f32[3,7,14]{2,1,0:T(8,128)S(1)}, u32[]{:S(2)}) copy-start(f32[3,7,14]{2,1,0:T(8,128)S(1)} %add_rsqrt_fusion.3) | copy-start | bytes 3532
  158.4 32.7 %copy-start.39 = (bf16[1,512,512]{2,1,0:T(8,128)(2,1)}, bf16[1,512,512]{2,1,0:T(8,128)(2,1)S(1)}, u32[]{:S(2)}) copy-start(bf16[1,512,512]{2,1,0:T(8,128)(2,1)S(1)} %all-gather.4) | copy-start | bytes 1572868
  200.1 6.2 collective-permute-start
  222.3 30.1 %copy-start.51 = (bf16[3,1,2,7,7,512]{5,2,4,3,0,1:T(2,128)(2,1)S(1)}, bf16[3,1,2,7,7,512]{5,2,4,3,0,1:T(2,128)(2,1)}, u32[]{:S(2)}) copy-start(bf16[3,1,2,7,7,512]{5,2,4,3,0,1:T(2,128)(2,1)} %copy-done.50) | copy-start | bytes 903172
  228.1 30.5 %collective-permute-start.1 = (bf16[3,3,14,512]{3,2,1,0:T(8,128)(2,1)}, bf16[3,3,14,512]{3,2,1,0:T(8,128)(2,1)}, u32[]{:S(2)}, u32[]{:S(2)}) collective-permute-start(bf16[3,3,14,512]{3,2,1,0:T(8,128)(2,1)} %pad_maximum_fusion.5), channel_id=1, source_target_pairs={{0,16},{16,0},{1,17},{17,1},{2,18},{18,2},{3,19},{19,3},{4,20},{20... | collective-permute-start | bytes 387080 | tf_op jit(solution)/shard_map/ppermute | solution.py:23
  276.2 6.3 collective-permute-start.2
  280.3 202.4 %reduce-scatter.13.cloned.1.call-start = ((), (), s32[]{:S(2)}) async-start(), calls=%async_computation.10 | async-start | bytes 1114112 | tf_op jit(solution)/shard_map/reduce_scatter | solution.py:367
  307.5 14.5 %collective-permute-start.3 = (bf16[3,3,14,512]{3,2,1,0:T(8,128)(2,1)S(1)}, bf16[3,3,14,512]{3,2,1,0:T(8,128)(2,1)S(1)}, u32[]{:S(2)}, u32[]{:S(2)}) collective-permute-start(bf16[3,3,14,512]{3,2,1,0:T(8,128)(2,1)S(1)} %fusion.117), channel_id=1, source_target_pairs={{0,16},{16,0},{1,17},{17,1},{2,18},{18,2},{3,19},{19,3},{4,20},{20... | collective-permute-start | bytes 387080 | tf_op jit(solution)/shard_map/ppermute | solution.py:23
  361.6 126.7 %copy-start.31 = (f32[3,1,7,2,7,512]{5,2,4,3,0,1:T(8,128)}, f32[3,1,7,2,7,512]{5,2,4,3,0,1:T(8,128)S(1)}, u32[]{:S(2)}) copy-start(f32[3,1,7,2,7,512]{5,2,4,3,0,1:T(8,128)S(1)} %copy.292) | copy-start | bytes 1806340
  428.4 139.6 %all-reduce.37.cloned.1.call-start = ((), (), s32[]{:S(2)}) async-start(), calls=%async_computation.22 | async-start | bytes 147456 | tf_op jit(solution)/shard_map/psum | solution.py:381
  484.2 95.9 %reduce-scatter.11.cloned.1.call-start = ((), (), s32[]{:S(2)}) async-start(), calls=%async_computation.9 | async-start | bytes 3342336 | tf_op jit(solution)/shard_map/reduce_scatter | solution.py:366
  488.2 160.9 %reduce-scatter.9.cloned.1.call-start = ((), (), s32[]{:S(2)}) async-start(), calls=%async_computation.8 | async-start | bytes 3342336 | tf_op jit(solution)/shard_map/reduce_scatter | solution.py:366
  496.8 227.8 %reduce-scatter.23.cloned.1.call-start = ((), (), s32[]{:S(2)}) async-start(), calls=%async_computation.15 | async-start | bytes 4456448 | tf_op jit(solution)/shard_map/reduce_scatter | solution.py:369
  501.6 298.7 %reduce-scatter.19.cloned.1.call-start = ((), (), s32[]{:S(2)}) async-start(), calls=%async_computation.13 | async-start | bytes 4456448 | tf_op jit(solution)/shard_map/reduce_scatter | solution.py:368
  506.6 369.1 %reduce-scatter.17.cloned.1.call-start = ((), (), s32[]{:S(2)}) async-start(), calls=%async_computation.12 | async-start | bytes 4456448 | tf_op jit(solution)/shard_map/reduce_scatter | solution.py:368
  511.7 439.6 %reduce-scatter.21.cloned.1.call-start = ((), (), s32[]{:S(2)}) async-start(), calls=%async_computation.14 | async-start | bytes 4456448 | tf_op jit(solution)/shard_map/reduce_scatter | solution.py:369
  516.5 469.9 %all-reduce.39.cloned.1.call-start = ((), (), s32[]{:S(2)}) async-start(), calls=%async_computation.23 | async-start | bytes 1441792 | tf_op jit(solution)/shard_map/psum | solution.py:380
  521.4 45.2 %copy-start.84 = (f32[3,7,14]{2,1,0:T(8,128)S(1)}, f32[3,7,14]{2,1,0:T(8,128)}, u32[]{:S(2)}) copy-start(f32[3,7,14]{2,1,0:T(8,128)} %get-tuple-element.23) | copy-start | bytes 3532
  521.4 45.2 %copy-start.30 = (f32[3,7,14,512]{3,2,1,0:T(8,128)S(1)}, f32[3,7,14,512]{3,2,1,0:T(8,128)}, u32[]{:S(2)}) copy-start(f32[3,7,14,512]{3,2,1,0:T(8,128)} %copy-done.29) | copy-start | bytes 1806340
  521.5 45.2 %copy-start.32 = (f32[3,1,7,2,7,512]{5,2,4,3,0,1:T(8,128)S(1)}, f32[3,1,7,2,7,512]{5,2,4,3,0,1:T(8,128)}, u32[]{:S(2)}) copy-start(f32[3,1,7,2,7,512]{5,2,4,3,0,1:T(8,128)} %copy-done.31) | copy-start | bytes 1806340
  568.0 384.9 %copy-start.133 = (bf16[1,64]{1,0:T(2,128)(2,1)S(1)}, bf16[1,64]{1,0:T(2,128)(2,1)}, u32[]{:S(2)}) copy-start(bf16[1,64]{1,0:T(2,128)(2,1)} %get-tuple-element.65) | copy-start | bytes 388
  568.0 384.9 %copy-start.134 = (bf16[1,64]{1,0:T(2,128)(2,1)S(1)}, bf16[1,64]{1,0:T(2,128)(2,1)}, u32[]{:S(2)}) copy-start(bf16[1,64]{1,0:T(2,128)(2,1)} %get-tuple-element.66) | copy-start | bytes 388
  568.0 385.5 %copy-start.131 = (bf16[1,32]{1,0:T(2,128)(2,1)S(1)}, bf16[1,32]{1,0:T(2,128)(2,1)}, u32[]{:S(2)}) copy-start(bf16[1,32]{1,0:T(2,128)(2,1)} %get-tuple-element.67) | copy-start | bytes 196
  568.0 385.5 %copy-start.132 = (bf16[1,32]{1,0:T(2,128)(2,1)S(1)}, bf16[1,32]{1,0:T(2,128)(2,1)}, u32[]{:S(2)}) copy-start(bf16[1,32]{1,0:T(2,128)(2,1)} %get-tuple-element.68) | copy-start | bytes 196
  568.0 386.0 %copy-start.129 = (bf16[1,32]{1,0:T(2,128)(2,1)S(1)}, bf16[1,32]{1,0:T(2,128)(2,1)}, u32[]{:S(2)}) copy-start(bf16[1,32]{1,0:T(2,128)(2,1)} %get-tuple-element.69) | copy-start | bytes 196
  568.0 386.0 %copy-start.130 = (bf16[1,32]{1,0:T(2,128)(2,1)S(1)}, bf16[1,32]{1,0:T(2,128)(2,1)}, u32[]{:S(2)}) copy-start(bf16[1,32]{1,0:T(2,128)(2,1)} %get-tuple-element.70) | copy-start | bytes 196
  568.0 386.6 %copy-start.127 = (bf16[1,32]{1,0:T(2,128)(2,1)S(1)}, bf16[1,32]{1,0:T(2,128)(2,1)}, u32[]{:S(2)}) copy-start(bf16[1,32]{1,0:T(2,128)(2,1)} %get-tuple-element.71) | copy-start | bytes 196
  568.0 386.6 %copy-start.128 = (bf16[1,32]{1,0:T(2,128)(2,1)S(1)}, bf16[1,32]{1,0:T(2,128)(2,1)}, u32[]{:S(2)}) copy-start(bf16[1,32]{1,0:T(2,128)(2,1)} %get-tuple-element.72) | copy-start | bytes 196
  568.1 387.2 %copy-start.125 = (bf16[1,128]{1,0:T(2,128)(2,1)S(1)}, bf16[1,128]{1,0:T(2,128)(2,1)}, u32[]{:S(2)}) copy-start(bf16[1,128]{1,0:T(2,128)(2,1)} %get-tuple-element.73) | copy-start | bytes 772
  568.1 387.2 %copy-start.126 = (bf16[1,128]{1,0:T(2,128)(2,1)S(1)}, bf16[1,128]{1,0:T(2,128)(2,1)}, u32[]{:S(2)}) copy-start(bf16[1,128]{1,0:T(2,128)(2,1)} %get-tuple-element.74) | copy-start | bytes 772
  568.1 387.7 %copy-start.123 = (bf16[1,32]{1,0:T(2,128)(2,1)S(1)}, bf16[1,32]{1,0:T(2,128)(2,1)}, u32[]{:S(2)}) copy-start(bf16[1,32]{1,0:T(2,128)(2,1)} %get-tuple-element.75) | copy-start | bytes 196
  568.1 387.7 %copy-start.124 = (bf16[1,32]{1,0:T(2,128)(2,1)S(1)}, bf16[1,32]{1,0:T(2,128)(2,1)}, u32[]{:S(2)}) copy-start(bf16[1,32]{1,0:T(2,128)(2,1)} %get-tuple-element.76) | copy-start | bytes 196
  568.1 388.3 %copy-start.86 = (bf16[1,32,512]{2,1,0:T(8,128)(2,1)S(1)}, bf16[1,32,512]{2,1,0:T(8,128)(2,1)}, u32[]{:S(2)}) copy-start(bf16[1,32,512]{2,1,0:T(8,128)(2,1)} %get-tuple-element.59) | copy-start | bytes 98308
  568.1 388.3 %copy-start.87 = (bf16[1,32,512]{2,1,0:T(8,128)(2,1)S(1)}, bf16[1,32,512]{2,1,0:T(8,128)(2,1)}, u32[]{:S(2)}) copy-start(bf16[1,32,512]{2,1,0:T(8,128)(2,1)} %get-tuple-element.60) | copy-start | bytes 98308
  580.0 411.7 %copy-start.1 = (s32[14,14]{1,0:T(8,128)S(1)}, s32[14,14]{1,0:T(8,128)}, u32[]{:S(2)}) copy-start(s32[14,14]{1,0:T(8,128)} %param.34) | copy-start | bytes 2356
  (122 other events, 423.0 us)
Sparse Core Ops, SparseCore 0:
  10.9 42.5 all-gather.30
  56.2 40.4 all-gather.32
  99.4 40.1 all-gather.34
  141.8 38.8 all-gather.36
  183.2 40.1 all-gather.38
  225.5 40.6 all-gather.40
  280.4 55.3 reduce-scatter.14
  428.6 54.1 reduce-scatter.12
  487.2 22.5 all-reduce.36
  513.5 66.5 reduce-scatter.10
  583.9 65.2 reduce-scatter.8
  652.9 71.6 reduce-scatter.22
  728.4 71.8 reduce-scatter.18
  804.0 71.7 reduce-scatter.16
  879.4 71.7 reduce-scatter.20
  954.3 32.0 all-reduce.38
where the time goes:
time: 1010 us; the launch traced here: 999 us
  waiting for transfers between devices  456 us (45%)
  blocking collectives  244 us (24%)
  local copies, waits for them, and re-layouts  129 us (13%)
  matrix products  89.4 us (9%)
  other arithmetic  56 us (6%)
  between operations  19.7 us (2%)
    reduce_scatter x2, waiting for transfers between devices, reduce_grads(): lax.psum_scatter(grads[2], 'dp', scatter_dimension=0, tiled=True)  148 us
    reduce_scatter x2, waiting for transfers between devices, reduce_grads(): lax.psum_scatter(grads[3], 'dp', scatter_dimension=0, tiled=True)  148 us
    unnamed x2, blocking collectives  123 us
    reduce_scatter x2, waiting for transfers between devices, reduce_grads(): lax.psum_scatter(grads[0], 'dp', scatter_dimension=0, tiled=True)  77 us
    reduce_scatter x2, waiting for transfers between devices, reduce_grads(): lax.psum_scatter(grads[1], 'dp', scatter_dimension=0, tiled=True)  44.8 us
    all_gather x2, blocking collectives, fetch_layer(): lax.all_gather(pieces[1], 'dp', axis=0, tiled=True)  43.6 us
    psum x1, blocking collectives, per_device(): table_total = lax.psum(jnp.stack(tables_all), ('rows', 'dp'))  42.1 us
    all_gather x2, blocking collectives, fetch_layer(): lax.all_gather(pieces[10], 'dp', axis=0, tiled=True)  36.3 us
  transfers between devices with their start and end apart: 20, of which 10 were waited for; matrix products, arithmetic and copies ran while one was open for 24% of the time, Pallas kernels for 0%

commit v1 on v0

v1 whole, which is shorter than its diff:
```python
import jax
import jax.numpy as jnp
from jax import lax
from jax.experimental import pallas as pl
from jax.experimental.pallas import tpu as pltpu
from jax.sharding import PartitionSpec as P

C = 512
HEADS = 16
HEAD_DIM = 32
WIN = 7
GRID = 14
SHIFT = 3
LAYERS = 2
REL = 169
SIDE = 8
PAD = SIDE * SIDE
LANES = 128
GROUP = LANES // HEAD_DIM
GROUPS = HEADS // GROUP


EPS = 1e-05
NEG = -1e30
SQRT_HALF = 0.7071067811865476
INV_ROOT_TAU = 0.3989422804014327


def swapped(array, axis, distance):
    return lax.ppermute(array, axis, [(i, i ^ 1 << distance) for i in range(lax.axis_size(axis))])


def product(spec, left, right):
    return jnp.einsum(spec, left, right, preferred_element_type=jnp.float32)


def outer(left, right):
    left_flat = left.reshape(-1, left.shape[-1])
    right_flat = right.reshape(-1, right.shape[-1])
    return lax.dot_general(
        left_flat, right_flat, (((0,), (0,)), ((), ())), preferred_element_type=jnp.float32
    )


def back_product(grad_rows, weight):
    return lax.dot_general(
        grad_rows,
        weight,
        (((grad_rows.ndim - 1,), (1,)), ((), ())),
        preferred_element_type=jnp.float32,
    )


def token_total(values):
    return jnp.sum(values.reshape(-1, values.shape[-1]), axis=0)


def to_padded(grid):
    images, _, cols, channels = grid.shape
    split = grid.reshape(images, WIN, cols // WIN, WIN, channels).transpose(0, 2, 1, 3, 4)
    padded = jnp.pad(split, ((0, 0), (0, 0), (0, SIDE - WIN), (0, SIDE - WIN), (0, 0)))
    return padded.reshape(-1, channels)


def from_padded(rows):
    channels = rows.shape[-1]
    split = rows.reshape(-1, GRID // WIN, SIDE, SIDE, channels)[:, :, :WIN, :WIN]
    return split.transpose(0, 2, 1, 3, 4).reshape(-1, WIN, GRID, channels)


def layernorm_apply(values, gain_vector, offset_vector):
    average = jnp.mean(values, axis=-1, keepdims=True)
    centered_input = values - average
    variance = jnp.mean(centered_input * centered_input, axis=-1, keepdims=True)
    inverse_deviation = lax.rsqrt(variance + EPS)
    standardized = centered_input * inverse_deviation
    return (standardized * gain_vector + offset_vector, standardized, inverse_deviation)


def layernorm_reverse(output_gradient, standardized, inverse_deviation, gain_vector):
    standardized_gradient = output_gradient * gain_vector
    input_gradient_rows = inverse_deviation * (
        standardized_gradient
        - jnp.mean(standardized_gradient, axis=-1, keepdims=True)
        - standardized * jnp.mean(standardized_gradient * standardized, axis=-1, keepdims=True)
    )
    return (
        input_gradient_rows,
        token_total(output_gradient * standardized),
        token_total(output_gradient),
    )


def gelu_value(preactivation):
    return preactivation * 0.5 * (1.0 + lax.erf(preactivation * SQRT_HALF))


def gelu_slope(preactivation):
    return (
        0.5 * (1.0 + lax.erf(preactivation * SQRT_HALF))
        + preactivation * jnp.exp(-0.5 * preactivation * preactivation) * INV_ROOT_TAU
    )


def head_lanes(dtype):
    shape = (GROUP, 1, LANES)
    head = lax.broadcasted_iota(jnp.int32, shape, 0)
    lane = lax.broadcasted_iota(jnp.int32, shape, 2)
    return (lane // HEAD_DIM == head).astype(jnp.float32).astype(dtype)


def spread(rows, lanes):
    return (rows[None] * lanes).reshape(GROUP * PAD, LANES)


def gather_heads(wide, lanes):
    return jnp.sum(wide.reshape(GROUP, PAD, LANES) * lanes, axis=0)


def dot_nt(left, right):
    return lax.dot_general(left, right, (((1,), (1,)), ((), ())), preferred_element_type=jnp.float32)


def dot_tn(left, right):
    return lax.dot_general(left, right, (((0,), (0,)), ((), ())), preferred_element_type=jnp.float32)


def window_probs(wide_query, keys, scores_bias):
    scores = dot_nt(wide_query, keys) + scores_bias
    weights = jnp.exp(scores - jnp.max(scores, axis=-1, keepdims=True))
    return weights / jnp.sum(weights, axis=-1, keepdims=True)


def attend_kernel(kinds, x_ref, w_ref, b_ref, sb_ref, packed_ref, context_ref):
    packed = jnp.dot(x_ref[...], w_ref[:, : 3 * C], preferred_element_type=jnp.float32)
    bias = b_ref[...]
    packed_ref[:, :C] = ((packed[:, :C] + bias[:, :C]) * HEAD_DIM ** (-0.5)).astype(jnp.bfloat16)
    packed_ref[:, C : 2 * C] = packed[:, C : 2 * C].astype(jnp.bfloat16)
    packed_ref[:, 2 * C :] = (packed[:, 2 * C :] + bias[:, C:]).astype(jnp.bfloat16)
    lanes = head_lanes(jnp.bfloat16)
    lanes_f32 = head_lanes(jnp.float32)

    def window(step, carry):
        rows = pl.ds(pl.multiple_of(step * PAD, PAD), PAD)
        kind = lax.rem(step, kinds)
        for group in range(GROUPS):
            low = group * LANES
            wide_query = spread(packed_ref[rows, low : low + LANES], lanes)
            keys = packed_ref[rows, C + low : C + low + LANES]
            values = packed_ref[rows, 2 * C + low : 2 * C + low + LANES]
            probs = window_probs(wide_query, keys, sb_ref[kind, group])
            wide = jnp.dot(
                probs.astype(jnp.bfloat16), values, preferred_element_type=jnp.float32
            )
            context_ref[rows, low : low + LANES] = gather_heads(wide, lanes_f32).astype(
                jnp.bfloat16
            )
        return carry

    lax.fori_loop(0, x_ref.shape[0] // PAD, window, 0)


def attend_back_kernel(kinds, packed_ref, dc_ref, sb_ref, dp_ref, db_ref, table_ref):
    lanes = head_lanes(jnp.bfloat16)
    lanes_f32 = head_lanes(jnp.float32)
    db_ref[...] = jnp.zeros_like(db_ref)
    table_ref[...] = jnp.zeros_like(table_ref)
    scale = HEAD_DIM ** (-0.5)

    def window(step, carry):
        rows = pl.ds(pl.multiple_of(step * PAD, PAD), PAD)
        kind = lax.rem(step, kinds)
        for group in range(GROUPS):
            low = group * LANES
            wide_query = spread(packed_ref[rows, low : low + LANES], lanes)
            keys = packed_ref[rows, C + low : C + low + LANES]
            values = packed_ref[rows, 2 * C + low : 2 * C + low + LANES]
            probs = window_probs(wide_query, keys, sb_ref[kind, group])
            wide_grad = spread(dc_ref[rows, low : low + LANES], lanes)
            grad_probs = dot_nt(wide_grad, values)
            grad_values = dot_tn(probs.astype(jnp.bfloat16), wide_grad)
            grad_scores = probs * (
                grad_probs - jnp.sum(probs * grad_probs, axis=-1, keepdims=True)
            )
            table_ref[group] += grad_scores
            scores_bf = grad_scores.astype(jnp.bfloat16)
            wide = jnp.dot(scores_bf, keys, preferred_element_type=jnp.float32)
            grad_query = gather_heads(wide, lanes_f32) * scale
            grad_keys = dot_tn(scores_bf, wide_query)
            dp_ref[rows, low : low + LANES] = grad_query.astype(jnp.bfloat16)
            dp_ref[rows, C + low : C + low + LANES] = grad_keys.astype(jnp.bfloat16)
            dp_ref[rows, 2 * C + low : 2 * C + low + LANES] = grad_values.astype(jnp.bfloat16)
            db_ref[:, low : low + LANES] += jnp.sum(grad_query, axis=0, keepdims=True)
            db_ref[:, C + low : C + low + LANES] += jnp.sum(grad_values, axis=0, keepdims=True)
        return carry

    lax.fori_loop(0, dc_ref.shape[0] // PAD, window, 0)


def in_vmem(count):
    return [pl.BlockSpec(memory_space=pltpu.VMEM)] * count


def attend(window_input, in_out_weight, in_bias, scores_bias):
    tokens = window_input.shape[0]
    kinds = scores_bias.shape[0]
    return pl.pallas_call(
        lambda *refs: attend_kernel(kinds, *refs),
        out_shape=(
            jax.ShapeDtypeStruct((tokens, 3 * C), jnp.bfloat16),
            jax.ShapeDtypeStruct((tokens, C), jnp.bfloat16),
        ),
        in_specs=in_vmem(4),
        out_specs=tuple(in_vmem(2)),
        cost_estimate=pl.CostEstimate(
            flops=8 * tokens * C * C, bytes_accessed=20 * 2**20, transcendentals=0
        ),
    )(window_input, in_out_weight, in_bias[None], scores_bias)


def attend_back(packed, grad_context, scores_bias):
    tokens = packed.shape[0]
    kinds = scores_bias.shape[0]
    return pl.pallas_call(
        lambda *refs: attend_back_kernel(kinds, *refs),
        out_shape=(
            jax.ShapeDtypeStruct((tokens, 3 * C), jnp.bfloat16),
            jax.ShapeDtypeStruct((1, 2 * C), jnp.float32),
            jax.ShapeDtypeStruct((GROUPS, GROUP * PAD, PAD), jnp.float32),
        ),
        in_specs=in_vmem(3),
        out_specs=tuple(in_vmem(3)),
        cost_estimate=pl.CostEstimate(
            flops=8 * tokens * C * C, bytes_accessed=40 * 2**20, transcendentals=0
        ),
    )(packed, grad_context, scores_bias)


def enter_grid(rows, shifted):
    if not shifted:
        return rows
    grid = from_padded(rows)
    incoming = swapped(grid[:, :SHIFT], "rows", 0)
    grid = jnp.concatenate([grid[:, SHIFT:], incoming], axis=1)
    return to_padded(jnp.roll(grid, -SHIFT, axis=2))


def leave_grid(rows, shifted):
    if not shifted:
        return rows
    grid = jnp.roll(from_padded(rows), SHIFT, axis=2)
    incoming = swapped(grid[:, WIN - SHIFT :].astype(jnp.bfloat16), "rows", 0).astype(grid.dtype)
    return to_padded(jnp.concatenate([incoming, grid[:, : WIN - SHIFT]], axis=1))


def layer_forward(stream, weights, vectors, scores_bias, shifted):
    in_out_weight, up_weight, down_weight = weights
    first_gain, first_offset, in_bias, out_bias = vectors[:4]
    second_gain, second_offset, up_bias, down_bias = vectors[4:]
    normalized, first_standardized, first_scale = layernorm_apply(stream, first_gain, first_offset)
    window_input = enter_grid(normalized.astype(jnp.bfloat16), shifted)
    packed, context = attend(window_input, in_out_weight, in_bias, scores_bias)
    local_context = leave_grid(context, shifted)
    attended = (
        stream
        + jnp.dot(local_context, in_out_weight[:, 3 * C :], preferred_element_type=jnp.float32)
        + out_bias
    )
    second_normalized, second_standardized, second_scale = layernorm_apply(
        attended, second_gain, second_offset
    )
    hidden = second_normalized.astype(jnp.bfloat16)
    preactivation = jnp.dot(hidden, up_weight, preferred_element_type=jnp.float32) + up_bias
    activated = gelu_value(preactivation).astype(jnp.bfloat16)
    result = (
        attended + jnp.dot(activated, down_weight, preferred_element_type=jnp.float32) + down_bias
    )
    kept = (
        first_standardized,
        first_scale,
        window_input,
        packed,
        local_context,
        second_standardized,
        second_scale,
        hidden,
        preactivation,
        activated,
    )
    return result, kept


def layer_backward(grad_flow, weights, vectors, scores_bias, onehot, shifted, kept):
    in_out_weight, up_weight, down_weight = weights
    first_gain, second_gain = vectors[0], vectors[4]
    (
        first_standardized,
        first_scale,
        window_input,
        packed,
        local_context,
        second_standardized,
        second_scale,
        hidden,
        preactivation,
        activated,
    ) = kept
    grad_bf = grad_flow.astype(jnp.bfloat16)
    grad_down = outer(activated, grad_bf)
    grad_down_bias = token_total(grad_flow)
    grad_pre = back_product(grad_bf, down_weight) * gelu_slope(preactivation)
    grad_pre_bf = grad_pre.astype(jnp.bfloat16)
    grad_up = outer(hidden, grad_pre_bf)
    grad_up_bias = token_total(grad_pre)
    attention_share, second_gain_gradient, second_offset_gradient = layernorm_reverse(
        back_product(grad_pre_bf, up_weight), second_standardized, second_scale, second_gain
    )
    mlp_shards = scatter_sum(owner_blocks((grad_up, grad_down)))
    grad_mixed = grad_flow + attention_share
    mixed_bf = grad_mixed.astype(jnp.bfloat16)
    grad_out = outer(local_context, mixed_bf)
    grad_out_bias = token_total(grad_mixed)
    grad_context = back_product(mixed_bf, in_out_weight[:, 3 * C :]).astype(jnp.bfloat16)
    grad_packed, grad_in_bias, table_term = attend_back(
        packed, enter_grid(grad_context, shifted), scores_bias
    )
    grad_in = outer(window_input, grad_packed)
    attn_shards = scatter_sum(owner_blocks((grad_in, grad_out)))
    normalized_gradient = leave_grid(
        back_product(grad_packed, in_out_weight[:, : 3 * C]), shifted
    )
    residual_share, first_gain_gradient, first_offset_gradient = layernorm_reverse(
        normalized_gradient, first_standardized, first_scale, first_gain
    )
    grad_table = lax.dot_general(
        onehot,
        table_term.reshape(HEADS, -1),
        (((0,), (1,)), ((), ())),
        precision=lax.Precision.HIGHEST,
    )
    vector_grads = (
        first_gain_gradient,
        first_offset_gradient,
        grad_in_bias.reshape(-1),
        grad_out_bias,
        second_gain_gradient,
        second_offset_gradient,
        grad_up_bias,
        grad_down_bias,
    )
    return grad_mixed + residual_share, mlp_shards, attn_shards, vector_grads, grad_table


def owner_blocks(grads):
    owners = lax.axis_size("dp")
    parts = []
    for grad in grads:
        depth = grad.shape[0] // owners
        blocks = grad.astype(jnp.bfloat16).reshape(owners, depth, -1, C).transpose(0, 2, 1, 3)
        parts.append(blocks.reshape(owners, -1, C))
    return jnp.concatenate(parts, axis=1)


def from_blocks(block, depth):
    return block.reshape(-1, depth, C).transpose(1, 0, 2).reshape(depth, -1)


def halve(array, axis_name, bit, dim):
    mine = (lax.axis_index(axis_name) >> bit) & 1
    keep = lax.dynamic_index_in_dim(array, mine, dim, keepdims=False)
    away = lax.dynamic_index_in_dim(array, 1 - mine, dim, keepdims=False)
    return add_bf(keep, swapped(away, axis_name, bit))


def add_bf(left, right):
    return (left.astype(jnp.float32) + right.astype(jnp.float32)).astype(jnp.bfloat16)


def halve_owner(blocks, bit):
    owners, rows, _ = blocks.shape
    return halve(blocks.reshape(owners // 2, 2, rows, C), "dp", bit, 1)


def halve_rows(blocks):
    owners, rows, _ = blocks.shape
    return halve(blocks.reshape(owners, 2, rows // 2, C), "rows", 0, 1)


def scatter_sum(blocks):
    bits = (lax.axis_size("dp") - 1).bit_length()
    blocks = halve_owner(blocks, 0)
    half = blocks.shape[1] // 2
    first, second = blocks[:, :half], blocks[:, half:]
    first, second = halve_owner(first, 1), halve_rows(second)
    first, second = halve_rows(first), halve_owner(second, 1)
    both = jnp.concatenate([first, second], axis=1)
    for bit in range(2, bits):
        both = halve_owner(both, bit)
    both = both[0].reshape(2, -1, C)
    other = swapped(both, "rows", 0)
    upper = lax.axis_index("rows") == 1
    low, high = jnp.where(upper, other, both), jnp.where(upper, both, other)
    return jnp.stack([low, high], axis=1).reshape(-1, C).astype(jnp.float32)


def gathered(piece):
    return lax.all_gather(piece, "dp", axis=0, tiled=True)


def per_device(
    images,
    cotangent,
    attn_in_weight,
    attn_out_weight,
    mlp_in_weight,
    mlp_out_weight,
    norm1_gain,
    norm1_bias,
    attn_in_bias,
    attn_out_bias,
    norm2_gain,
    norm2_bias,
    mlp_in_bias,
    mlp_out_bias,
    bias_table,
    region_labels,
    table_index,
):
    owners = lax.axis_size("dp")
    vector_shards = (
        norm1_gain,
        norm1_bias,
        attn_in_bias,
        attn_out_bias,
        norm2_gain,
        norm2_bias,
        mlp_in_bias,
        mlp_out_bias,
    )
    widths = [member.shape[1] for member in vector_shards]
    vector_all = gathered(jnp.concatenate(vector_shards, axis=1).reshape(1, -1))
    vector_all = vector_all.reshape(owners, LAYERS, -1).astype(jnp.float32)

    def layer_vectors(layer_no):
        start, result = 0, []
        for width in widths:
            result.append(vector_all[:, layer_no, start : start + width].reshape(-1))
            start += width
        return tuple(result)

    def layer_weights(layer_no):
        in_out = jnp.concatenate([attn_in_weight[layer_no], attn_out_weight[layer_no]], axis=1)
        return gathered(in_out), gathered(mlp_in_weight[layer_no]), gathered(mlp_out_weight[layer_no])

    def pad_window(values, fill):
        grid = values.reshape(values.shape[:-1] + (WIN, WIN))
        pads = [(0, 0)] * (values.ndim - 1) + [(0, SIDE - WIN)] * 2
        return jnp.pad(grid, pads, constant_values=fill).reshape(values.shape[:-1] + (PAD,))

    def pad_pair(values, fill):
        both = pad_window(jnp.swapaxes(pad_window(values, fill), -1, -2), fill)
        return jnp.swapaxes(both, -1, -2)

    half_index = lax.axis_index("rows")
    local_labels = lax.dynamic_slice_in_dim(region_labels, half_index * WIN, WIN, 0)
    label_tiles = (
        local_labels.reshape(WIN, GRID // WIN, WIN).transpose(1, 0, 2).reshape(GRID // WIN, -1)
    )
    same = label_tiles[:, :, None] == label_tiles[:, None, :]
    real_key = pad_window(jnp.ones((WIN * WIN,), jnp.int32), 0) == 1
    allowed_pair = (
        jnp.broadcast_to(real_key[None, None, :], (1, PAD, PAD)),
        (pad_pair(same.astype(jnp.int32), 1) == 1) & real_key[None, None, :],
    )
    index_pad = pad_pair(table_index, 0)
    onehot = (index_pad.reshape(-1)[:, None] == jnp.arange(REL, dtype=jnp.int32)[None, :]).astype(
        jnp.float32
    )

    def scores_bias_of(layer_no):
        picked = jnp.take(bias_table[layer_no], index_pad.reshape(-1), axis=0).T
        picked = picked.reshape(HEADS, PAD, PAD)
        allowed = allowed_pair[layer_no % 2]
        masked = jnp.where(allowed[:, None], picked[None], NEG)
        return masked.reshape(-1, GROUPS, GROUP * PAD, PAD)

    stream = to_padded(images).astype(jnp.float32)
    weights = [layer_weights(layer_no) for layer_no in range(LAYERS)]
    vectors = [layer_vectors(layer_no) for layer_no in range(LAYERS)]
    score_biases = [scores_bias_of(layer_no) for layer_no in range(LAYERS)]
    kept_all = []
    for layer_no in range(LAYERS):
        stream, kept = layer_forward(
            stream, weights[layer_no], vectors[layer_no], score_biases[layer_no], layer_no % 2 == 1
        )
        kept_all.append(kept)
    final_out = from_padded(stream.astype(jnp.bfloat16))
    grad_flow = to_padded(cotangent).astype(jnp.float32)
    mlp_all, attn_all, vectors_all, tables_all = ([None] * LAYERS for _ in range(4))
    for layer_no in reversed(range(LAYERS)):
        grad_flow, mlp_all[layer_no], attn_all[layer_no], grads, tables_all[layer_no] = (
            layer_backward(
                grad_flow,
                weights[layer_no],
                vectors[layer_no],
                score_biases[layer_no],
                onehot,
                layer_no % 2 == 1,
                kept_all[layer_no],
            )
        )
        vectors_all[layer_no] = jnp.concatenate(grads)
    lengths = [width * owners for width in widths]
    small = jnp.concatenate(vectors_all + [jnp.stack(tables_all).reshape(-1)])
    total = small.shape[0]
    small = jnp.pad(small, (0, -total % (8 * LANES))).reshape(-1, LANES)
    small = lax.psum(small, ("rows", "dp")).reshape(-1)[:total]
    vector_total = small[: LAYERS * sum(lengths)].reshape(LAYERS, -1)
    table_total = small[LAYERS * sum(lengths) :].reshape(bias_table.shape)
    vector_outs, start = [], 0
    owner = lax.axis_index("dp")
    for width, length in zip(widths, lengths):
        part = vector_total[:, start : start + length]
        vector_outs.append(lax.dynamic_slice_in_dim(part, owner * width, width, 1))
        start += length
    depth = attn_in_weight.shape[1]

    def stacked(blocks, low, high, rows):
        return jnp.stack([from_blocks(block[low * depth : high * depth], rows) for block in blocks])

    down_depth = mlp_out_weight.shape[1]
    up_blocks = mlp_in_weight.shape[2] // C
    grad_up = stacked(mlp_all, 0, up_blocks, depth)
    grad_down = jnp.stack([block[up_blocks * depth :].reshape(down_depth, C) for block in mlp_all])
    grad_in = stacked(attn_all, 0, 3, depth)
    grad_out = stacked(attn_all, 3, 4, depth)
    return (
        final_out,
        from_padded(grad_flow),
        grad_in,
        grad_out,
        grad_up,
        grad_down,
        *vector_outs,
        table_total,
    )


def solution(mesh):
    return jax.shard_map(
        per_device,
        mesh=mesh,
        in_specs=(
            P("dp", "rows", None, None),
            P("dp", "rows", None, None),
            P(None, "dp", None),
            P(None, "dp", None),
            P(None, "dp", None),
            P(None, "dp", None),
            P(None, "dp"),
            P(None, "dp"),
            P(None, "dp"),
            P(None, "dp"),
            P(None, "dp"),
            P(None, "dp"),
            P(None, "dp"),
            P(None, "dp"),
            P(),
            P(),
            P(),
        ),
        out_specs=(
            P("dp", "rows", None, None),
            P("dp", "rows", None, None),
            P(None, "dp", None),
            P(None, "dp", None),
            P(None, "dp", None),
            P(None, "dp", None),
            P(None, "dp"),
            P(None, "dp"),
            P(None, "dp"),
            P(None, "dp"),
            P(None, "dp"),
            P(None, "dp"),
            P(None, "dp"),
            P(None, "dp"),
            P(),
        ),
        check_vma=False,
    )
```

time: 1010 us -> 641 us (0.63)
  blocking collectives: 244 us -> 23.3 us
  waiting for transfers between devices: 456 us -> 311 us
  Pallas kernels: 0 us -> 47.5 us
  starting transfers between devices: 4.4 us -> 38.8 us
  matrix products: 89.4 us -> 59.1 us
  local copies, waits for them, and re-layouts: 129 us -> 106 us
  other arithmetic: 56 us -> 34.6 us
    reduce_scatter x8 -> x0, waiting for transfers between devices: 418 us -> none  [the longest x2 148 us: reduce_grads(): lax.psum_scatter(grads[2], 'dp', scatter_dimension=0, tiled=True)]
    all_gather x6, waiting for transfers between devices: 0.11 us -> 131 us  [gathered(): return lax.all_gather(piece, 'dp', axis=0, tiled=True)]
    unnamed x2 -> x0, blocking collectives: 123 us -> none
    psum x2 -> x1, waiting for transfers between devices: 29.4 us -> 106 us  [per_device(): small = lax.psum(small, ('rows', 'dp')).reshape(-1)[:total]]
    ppermute x4 -> x36, waiting for transfers between devices: 7.43 us -> 72.1 us  [swapped(): lax.ppermute(array, axis, [(i, i ^ 1 << distance) for i in range(lax.axis...]
    all_gather x4 -> x1, blocking collectives: 79.9 us -> 23.3 us  [gathered(): return lax.all_gather(piece, 'dp', axis=0, tiled=True)]
    pallas_call x0 -> x4, Pallas kernels: none -> 47.5 us  [the longest x2 30.2 us: attend_back(): pl.pallas_call(lambda *refs: attend_back_kernel(kinds, *refs), out_shape=...]
    psum x1 -> x0, blocking collectives: 42.1 us -> none  [per_device(): table_total = lax.psum(jnp.stack(tables_all), ('rows', 'dp'))]
  transfers between devices with their start and end apart: 20 -> 43, of which waited for: 10 -> 32; matrix products, arithmetic and copies ran while one was open for 24% -> 26% of each run, Pallas kernels for 0% -> 7%
where the time goes in v1:
time: 641 us; the launch traced here: 636 us
  waiting for transfers between devices  311 us (49%)
  local copies, waits for them, and re-layouts  106 us (17%)
  matrix products  59.1 us (9%)
  Pallas kernels  47.5 us (7%)
  starting transfers between devices  38.8 us (6%)
  other arithmetic  34.6 us (5%)
  blocking collectives  23.3 us (4%)
  between operations  16.3 us (3%)
    all_gather x6, waiting for transfers between devices, gathered(): return lax.all_gather(piece, 'dp', axis=0, tiled=True)  131 us
    psum x1, waiting for transfers between devices, per_device(): small = lax.psum(small, ('rows', 'dp')).reshape(-1)[:total]  106 us
    ppermute x36, waiting for transfers between devices, swapped(): lax.ppermute(array, axis, [(i, i ^ 1 << distance) for i in range(lax.axis...  72.1 us
    ppermute x36, starting transfers between devices, swapped(): lax.ppermute(array, axis, [(i, i ^ 1 << distance) for i in range(lax.axis...  38.5 us
    pallas_call x2, Pallas kernels, attend_back(): pl.pallas_call(lambda *refs: attend_back_kernel(kinds, *refs), out_shape=...  30.2 us
    gather x2, local copies, waits for them, and re-layouts, scores_bias_of(): picked = jnp.take(bias_table[layer_no], index_pad.reshape(-1), axis=0).T  28.8 us
    reshape x6, local copies, waits for them, and re-layouts, owner_blocks(): grad.astype(jnp.bfloat16).reshape(owners, depth, -1, C)  26.5 us
    all_gather x1, blocking collectives, gathered(): return lax.all_gather(piece, 'dp', axis=0, tiled=True)  23.3 us
  transfers between devices with their start and end apart: 43, of which 32 were waited for; matrix products, arithmetic and copies ran while one was open for 26% of the time, Pallas kernels for 7%

profile of v1, /device:TPU:0, one launch (start us, length us, event | category | flops | bytes accessed | tf_op | source)
XLA Modules:
  0.0 636.1 jit_solution(2857951127691717095)
XLA Ops:
  15.9 23.3 %all-gather.4 = bf16[16,1,768]{2,1,0:T(2,128)(2,1)S(1)} all-gather(bf16[1,1,768]{2,1,0:T(2,128)(2,1)S(1)} %reshape.660), channel_id=1, replica_groups=mesh['rows'=2,'dp'=16] {'dp'}, dimensions={0}, use_global_device_ids=true | all-gather | bytes 26112 | tf_op jit(solution)/shard_map/all_gather | solution.py:407
  45.8 14.6 %gather_fusion = f32[4096,16]{1,0:T(8,128)} fusion(f32[169,16]{1,0:T(8,128)S(1)} %bitcast.428, s32[4096]{0:T(1024)S(1)} %fusion.117), kind=kCustom, calls=%fused_computation.clone | custom fusion | bytes 540672 | tf_op jit(solution)/shard_map/jit(_take)/gather | solution.py:481
  60.4 14.2 %gather_fusion.1 = f32[4096,16]{1,0:T(8,128)} fusion(f32[169,16]{1,0:T(8,128)S(1)} %bitcast.427, s32[4096]{0:T(1024)S(1)} %fusion.117), kind=kCustom, calls=%fused_computation.1.clone | custom fusion | bytes 540672 | tf_op jit(solution)/shard_map/jit(_take)/gather | solution.py:481
  74.6 3.5 select_bitcast_fusion
  78.1 2.9 copy.206
  86.4 8.6 %shard_map.280 = (bf16[384,1536]{1,0:T(8,128)(2,1)}, bf16[384,512]{1,0:T(8,128)(2,1)}) custom-call(bf16[384,512]{1,0:T(8,128)(2,1)} %add_convert_fusion.3.refs_0_, bf16[512,2048]{1,0:T(8,128)(2,1)} %all-gather.12.cloned.1.call-done.refs_1_, f32[1,1024]{1,0:T(1,128)} %broadcast_in_dim_reshape_squeeze.4.refs_2_, ...), custom_call_target="tpu_custom_call" | custom-call | flops 805306368 | bytes 20971520 | tf_op jit(solution)/shard_map/pallas_call | solution.py:207
  98.4 4.8 multiply_convert_fusion.1
  103.2 38.1 %all-gather.18.cloned.1.call-done = bf16[1,2048,512]{2,1,0:T(8,128)(2,1)} async-done(((bf16[1,128,512]{2,1,0:T(8,128)(2,1)}), bf16[1,2048,512]{2,1,0:T(8,128)(2,1)}) %all-gather.18.cloned.1.call-update) | async-done | bytes 2097168 | tf_op jit(solution)/shard_map/all_gather | solution.py:407
  141.2 3.1 fusion.133
  148.5 3.1 collective-permute-done
  152.8 30.6 %all-gather.14.cloned.1.call-done.refs_1_ = bf16[512,2048]{1,0:T(8,128)(2,1)} async-done(((bf16[32,2048]{1,0:T(8,128)(2,1)}), bf16[512,2048]{1,0:T(8,128)(2,1)}) %all-gather.14.cloned.1.call-update) | async-done | bytes 2097168 | tf_op jit(solution)/shard_map/all_gather | solution.py:407
  183.5 8.7 %shard_map.281 = (bf16[384,1536]{1,0:T(8,128)(2,1)}, bf16[384,512]{1,0:T(8,128)(2,1)}) custom-call(bf16[384,512]{1,0:T(8,128)(2,1)} %bitcast.461, bf16[512,2048]{1,0:T(8,128)(2,1)} %all-gather.14.cloned.1.call-done.refs_1_, f32[1,1024]{1,0:T(1,128)} %broadcast_in_dim_reshape_squeeze.5.refs_2_, f32[2,4,256,64]{3,2,1,0:T(8,128)} %bitcast_select_fusion.refs_3_.refs_2_), custom_call_target="tpu_custom_call" | custom-call | flops 805306368 | bytes 20971520 | tf_op jit(solution)/shard_map/pallas_call | solution.py:207
  195.9 4.2 collective-permute-done.1
  202.3 23.3 %all-gather.20.cloned.1.call-done = bf16[1,512,2048]{2,1,0:T(8,128)(2,1)} async-done(((bf16[1,32,2048]{2,1,0:T(8,128)(2,1)}), bf16[1,512,2048]{2,1,0:T(8,128)(2,1)}) %all-gather.20.cloned.1.call-update) | async-done | bytes 2097168 | tf_op jit(solution)/shard_map/all_gather | solution.py:407
  225.6 4.7 multiply_convert_fusion
  230.4 37.5 %all-gather.22.cloned.1.call-done = bf16[1,2048,512]{2,1,0:T(8,128)(2,1)} async-done(((bf16[1,128,512]{2,1,0:T(8,128)(2,1)}), bf16[1,2048,512]{2,1,0:T(8,128)(2,1)}) %all-gather.22.cloned.1.call-update) | async-done | bytes 2097168 | tf_op jit(solution)/shard_map/all_gather | solution.py:407
  267.9 4.9 fusion.136
  272.8 2.8 convolution_convert_fusion.1
  281.5 2.7 convolution_convert_fusion
  286.1 4.5 reshape.595
  296.0 3.5 collective-permute-done.2
  300.7 15.2 %shard_map.282 = (bf16[384,1536]{1,0:T(8,128)(2,1)}, f32[1,1024]{1,0:T(1,128)}, f32[4,256,64]{2,1,0:T(8,128)}) custom-call(bf16[384,1536]{1,0:T(8,128)(2,1)} %get-tuple-element.28.refs_0_, bf16[384,512]{1,0:T(8,128)(2,1)} %bitcast.537, f32[2,4,256,64]{3,2,1,0:T(8,128)} %bitcast_select_fusion.refs_3_.refs_2_), custom_call_target="tpu_custom_call" | custom-call | flops 805306368 | bytes 41943040 | tf_op jit(solution)/shard_map/pallas_call | solution.py:224
  315.9 2.6 fusion.38
  326.3 5.9 reshape.581
  342.7 2.7 convolution_convert_fusion.2
  346.2 2.6 fusion.135
  348.8 2.7 convolution_convert_fusion.3
  351.6 2.6 multiply_reduce_fusion.1
  354.2 4.5 reshape.588
  358.6 3.7 copy.230
  366.0 15.0 %shard_map.283 = (bf16[384,1536]{1,0:T(8,128)(2,1)}, f32[1,1024]{1,0:T(1,128)}, f32[4,256,64]{2,1,0:T(8,128)}) custom-call(bf16[384,1536]{1,0:T(8,128)(2,1)} %get-tuple-element.30.refs_0_, bf16[384,512]{1,0:T(8,128)(2,1)} %convolution_convert_fusion.8.refs_1_, f32[1,4,256,64]{3,2,1,0:T(8,128)} %broadcast_select_fusion.refs_3_.refs_2_), custom_call_target="tpu_custom_call" | custom-call | flops 805306368 | bytes 41943040 | tf_op jit(solution)/shard_map/pallas_call | solution.py:224
  381.1 3.7 convolution_convert_fusion.5
  384.8 2.9 multiply_reduce_fusion.2
  393.7 5.6 reshape.574
  405.9 106.3 %all-reduce.14.cloned.1.call-done = f32[144,128]{1,0:T(8,128)} async-done(((f32[144,128]{1,0:T(8,128)}), f32[144,128]{1,0:T(8,128)}) %all-reduce.14.cloned.1.call-update) | async-done | bytes 73744 | tf_op jit(solution)/shard_map/psum | solution.py:517
  526.9 3.6 collective-permute-done.13
  532.9 3.2 collective-permute-done.5
  544.9 2.5 collective-permute-done.8
  550.8 2.6 collective-permute-start.9
  559.7 2.7 collective-permute-done.10
  563.5 3.2 collective-permute-done.11
  567.9 2.5 fusion
  577.5 7.9 %collective-permute-done.29 = bf16[4,128,512]{2,1,0:T(8,128)(2,1)S(1)} collective-permute-done((bf16[4,128,512]{2,1,0:T(8,128)(2,1)S(1)}, bf16[4,128,512]{2,1,0:T(8,128)(2,1)S(1)}, u32[]{:S(2)}, u32[]{:S(2)}) %collective-permute-start.29) | collective-permute-done | bytes 524320 | tf_op jit(solution)/shard_map/ppermute | solution.py:30
  587.9 6.9 %collective-permute-done.21 = bf16[4,128,512]{2,1,0:T(8,128)(2,1)S(1)} collective-permute-done((bf16[4,128,512]{2,1,0:T(8,128)(2,1)S(1)}, bf16[4,128,512]{2,1,0:T(8,128)(2,1)S(1)}, u32[]{:S(2)}, u32[]{:S(2)}) %collective-permute-start.21) | collective-permute-done | bytes 524320 | tf_op jit(solution)/shard_map/ppermute | solution.py:30
  609.2 3.8 collective-permute-done.34
  615.2 2.9 collective-permute-done.35
  618.2 3.6 collective-permute-done.26
  623.4 3.5 collective-permute-done.27
  (509 shorter events, 151.3 us)
Async XLA Ops:
  7.3 79.1 %all-gather.12.cloned.1.call-start = ((), (), s32[]{:S(2)}) async-start(), calls=%async_computation | async-start | bytes 2228224 | tf_op jit(solution)/shard_map/all_gather | solution.py:407
  9.9 88.5 %all-gather.16.cloned.1.call-start = ((), (), s32[]{:S(2)}) async-start(), calls=%async_computation.3 | async-start | bytes 2228224 | tf_op jit(solution)/shard_map/all_gather | solution.py:407
  11.6 129.6 %all-gather.18.cloned.1.call-start = ((), (), s32[]{:S(2)}) async-start(), calls=%async_computation.4 | async-start | bytes 2228224 | tf_op jit(solution)/shard_map/all_gather | solution.py:407
  13.4 170.1 %all-gather.14.cloned.1.call-start = ((), (), s32[]{:S(2)}) async-start(), calls=%async_computation.1 | async-start | bytes 2228224 | tf_op jit(solution)/shard_map/all_gather | solution.py:407
  14.1 211.5 %all-gather.20.cloned.1.call-start = ((), (), s32[]{:S(2)}) async-start(), calls=%async_computation.5 | async-start | bytes 2228224 | tf_op jit(solution)/shard_map/all_gather | solution.py:407
  14.7 253.2 %all-gather.22.cloned.1.call-start = ((), (), s32[]{:S(2)}) async-start(), calls=%async_computation.6 | async-start | bytes 2228224 | tf_op jit(solution)/shard_map/all_gather | solution.py:407
  15.3 496.8 %all-reduce.14.cloned.1.call-start = ((), (), s32[]{:S(2)}) async-start(), calls=%async_computation.2 | async-start | bytes 147456 | tf_op jit(solution)/shard_map/psum | solution.py:517
  44.4 41.1 %copy-start.35 = (f32[512]{0:T(512)}, f32[512]{0:T(512)S(1)}, u32[]{:S(2)}) copy-start(f32[512]{0:T(512)S(1)} %mul.270) | copy-start | bytes 6148
  44.5 53.9 %copy-start.55 = (f32[512]{0:T(512)}, f32[512]{0:T(512)S(1)}, u32[]{:S(2)}) copy-start(f32[512]{0:T(512)S(1)} %add.401) | copy-start | bytes 6148
  45.8 49.2 %copy-start.7 = (f32[3,2,8,8,512]{4,3,2,1,0:T(8,128)}, f32[3,2,8,8,512]{4,3,2,1,0:T(8,128)S(1)}, u32[]{:S(2)}) copy-start(f32[3,2,8,8,512]{4,3,2,1,0:T(8,128)S(1)} %copy.193) | copy-start | bytes 2359300
  96.6 44.6 %copy-start.14 = (f32[384,512]{1,0:T(8,128)}, f32[384,512]{1,0:T(8,128)S(1)}, u32[]{:S(2)}) copy-start(f32[384,512]{1,0:T(8,128)S(1)} %get-tuple-element.173) | copy-start | bytes 2359300
  145.1 6.6 %collective-permute-start = (bf16[3,3,14,512]{3,1,2,0:T(4,128)(2,1)S(1)}, bf16[3,3,14,512]{3,1,2,0:T(4,128)(2,1)S(1)}, u32[]{:S(2)}, u32[]{:S(2)}) collective-permute-start(bf16[3,3,14,512]{3,1,2,0:T(4,128)(2,1)S(1)} %slice.350), channel_id=1, source_target_pairs={{0,16},{16,0},{1,17},{17,1},{2,18},{18,2},{3,19},{19,3},{4,20},{20... | collective-permute-start | bytes 387080 | tf_op jit(solution)/shard_map/ppermute | solution.py:30
  193.6 6.6 %collective-permute-start.1 = (bf16[3,3,14,512]{3,1,2,0:T(4,128)(2,1)S(1)}, bf16[3,3,14,512]{3,1,2,0:T(4,128)(2,1)S(1)}, u32[]{:S(2)}, u32[]{:S(2)}) collective-permute-start(bf16[3,3,14,512]{3,1,2,0:T(4,128)(2,1)S(1)} %fusion.113), channel_id=1, source_target_pairs={{0,16},{16,0},{1,17},{17,1},{2,18},{18,2},{3,19},{19,3},{4,20},{20... | collective-permute-start | bytes 387080 | tf_op jit(solution)/shard_map/ppermute | solution.py:30
  293.0 6.6 %collective-permute-start.2 = (bf16[3,3,14,512]{3,1,2,0:T(4,128)(2,1)S(1)}, bf16[3,3,14,512]{3,1,2,0:T(4,128)(2,1)S(1)}, u32[]{:S(2)}, u32[]{:S(2)}) collective-permute-start(bf16[3,3,14,512]{3,1,2,0:T(4,128)(2,1)S(1)} %slice.368), channel_id=1, source_target_pairs={{0,16},{16,0},{1,17},{17,1},{2,18},{18,2},{3,19},{19,3},{4,20},{20... | collective-permute-start | bytes 387080 | tf_op jit(solution)/shard_map/ppermute | solution.py:30
  296.0 271.9 %collective-permute-start.28 = (bf16[8,256,512]{2,1,0:T(8,128)(2,1)}, bf16[8,256,512]{2,1,0:T(8,128)(2,1)}, u32[]{:S(2)}, u32[]{:S(2)}) collective-permute-start(bf16[8,256,512]{2,1,0:T(8,128)(2,1)} %fusion.15), channel_id=1, source_target_pairs={{0,1},{1,0},{2,3},{3,2},{4,5},{5,4},{6,7},{7,6},{8,9},{9,8},{10,11... | collective-permute-start | bytes 6291464 | tf_op jit(solution)/shard_map/ppermute | solution.py:30
  322.9 14.0 %collective-permute-start.3 = (bf16[3,3,14,512]{3,1,2,0:T(4,128)(2,1)}, bf16[3,3,14,512]{3,1,2,0:T(4,128)(2,1)}, u32[]{:S(2)}, u32[]{:S(2)}) collective-permute-start(bf16[3,3,14,512]{3,1,2,0:T(4,128)(2,1)} %fusion.95), channel_id=1, source_target_pairs={{0,16},{16,0},{1,17},{17,1},{2,18},{18,2},{3,19},{19,3},{4,20},{20... | collective-permute-start | bytes 387080 | tf_op jit(solution)/shard_map/ppermute | solution.py:30
  335.5 184.1 %collective-permute-start.12 = (bf16[8,128,512]{2,1,0:T(8,128)(2,1)}, bf16[8,128,512]{2,1,0:T(8,128)(2,1)}, u32[]{:S(2)}, u32[]{:S(2)}) collective-permute-start(bf16[8,128,512]{2,1,0:T(8,128)(2,1)} %fusion.62), channel_id=1, source_target_pairs={{0,1},{1,0},{2,3},{3,2},{4,5},{5,4},{6,7},{7,6},{8,9},{9,8},{10,11... | collective-permute-start | bytes 3145736 | tf_op jit(solution)/shard_map/ppermute | solution.py:30
  403.8 120.2 %collective-permute-start.4 = (bf16[8,128,512]{2,1,0:T(8,128)(2,1)}, bf16[8,128,512]{2,1,0:T(8,128)(2,1)}, u32[]{:S(2)}, u32[]{:S(2)}) collective-permute-start(bf16[8,128,512]{2,1,0:T(8,128)(2,1)} %fusion.66), channel_id=1, source_target_pairs={{0,1},{1,0},{2,3},{3,2},{4,5},{5,4},{6,7},{7,6},{8,9},{9,8},{10,11... | collective-permute-start | bytes 3145736 | tf_op jit(solution)/shard_map/ppermute | solution.py:30
  404.4 115.2 %copy-start.19 = (bf16[512,512]{1,0:T(8,128)(2,1)S(1)}, bf16[512,512]{1,0:T(8,128)(2,1)}, u32[]{:S(2)}) copy-start(bf16[512,512]{1,0:T(8,128)(2,1)} %convolution_convert_fusion.6) | copy-start | bytes 1572868
  405.8 166.7 %collective-permute-start.20 = (bf16[8,256,512]{2,1,0:T(8,128)(2,1)}, bf16[8,256,512]{2,1,0:T(8,128)(2,1)}, u32[]{:S(2)}, u32[]{:S(2)}) collective-permute-start(bf16[8,256,512]{2,1,0:T(8,128)(2,1)} %fusion.19), channel_id=1, source_target_pairs={{0,1},{1,0},{2,3},{3,2},{4,5},{5,4},{6,7},{7,6},{8,9},{9,8},{10,11... | collective-permute-start | bytes 6291464 | tf_op jit(solution)/shard_map/ppermute | solution.py:30
  521.5 9.0 %collective-permute-start.13 = (bf16[4,64,512]{2,1,0:T(8,128)(2,1)S(1)}, bf16[4,64,512]{2,1,0:T(8,128)(2,1)S(1)}, u32[]{:S(2)}, u32[]{:S(2)}) collective-permute-start(bf16[4,64,512]{2,1,0:T(8,128)(2,1)S(1)} %dynamic-slice_bitcast_fusion.11), channel_id=1, source_target_pairs={{0,2},{1,3},{2,0},{3,1},{4,6},{5,7},{6,4},{7,5},{8,10},{9,11},{10,... | collective-permute-start | bytes 786440 | tf_op jit(solution)/shard_map/ppermute | solution.py:30
  523.0 9.2 %collective-permute-start.15 = (bf16[8,32,512]{2,1,0:T(8,128)(2,1)S(1)}, bf16[8,32,512]{2,1,0:T(8,128)(2,1)S(1)}, u32[]{:S(2)}, u32[]{:S(2)}) collective-permute-start(bf16[8,32,512]{2,1,0:T(8,128)(2,1)S(1)} %dynamic-slice_bitcast_fusion.10), channel_id=1, source_target_pairs={{0,16},{16,0},{1,17},{17,1},{2,18},{18,2},{3,19},{19,3},{4,20},{20... | collective-permute-start | bytes 786440 | tf_op jit(solution)/shard_map/ppermute | solution.py:30
  525.7 10.5 %collective-permute-start.5 = (bf16[4,64,512]{2,1,0:T(8,128)(2,1)S(1)}, bf16[4,64,512]{2,1,0:T(8,128)(2,1)S(1)}, u32[]{:S(2)}, u32[]{:S(2)}) collective-permute-start(bf16[4,64,512]{2,1,0:T(8,128)(2,1)S(1)} %dynamic-slice_bitcast_fusion.13), channel_id=1, source_target_pairs={{0,2},{1,3},{2,0},{3,1},{4,6},{5,7},{6,4},{7,5},{8,10},{9,11},{10,... | collective-permute-start | bytes 786440 | tf_op jit(solution)/shard_map/ppermute | solution.py:30
  530.5 9.2 %collective-permute-start.7 = (bf16[8,32,512]{2,1,0:T(8,128)(2,1)S(1)}, bf16[8,32,512]{2,1,0:T(8,128)(2,1)S(1)}, u32[]{:S(2)}, u32[]{:S(2)}) collective-permute-start(bf16[8,32,512]{2,1,0:T(8,128)(2,1)S(1)} %dynamic-slice_bitcast_fusion.12), channel_id=1, source_target_pairs={{0,16},{16,0},{1,17},{17,1},{2,18},{18,2},{3,19},{19,3},{4,20},{20... | collective-permute-start | bytes 786440 | tf_op jit(solution)/shard_map/ppermute | solution.py:30
  532.2 10.2 %collective-permute-start.14 = (bf16[4,32,512]{2,1,0:T(8,128)(2,1)S(1)}, bf16[4,32,512]{2,1,0:T(8,128)(2,1)S(1)}, u32[]{:S(2)}, u32[]{:S(2)}) collective-permute-start(bf16[4,32,512]{2,1,0:T(8,128)(2,1)S(1)} %dynamic-slice_bitcast_fusion.16), channel_id=1, source_target_pairs={{0,16},{16,0},{1,17},{17,1},{2,18},{18,2},{3,19},{19,3},{4,20},{20... | collective-permute-start | bytes 393224 | tf_op jit(solution)/shard_map/ppermute | solution.py:30
  536.1 7.9 %collective-permute-start.16 = (bf16[4,32,512]{2,1,0:T(8,128)(2,1)S(1)}, bf16[4,32,512]{2,1,0:T(8,128)(2,1)S(1)}, u32[]{:S(2)}, u32[]{:S(2)}) collective-permute-start(bf16[4,32,512]{2,1,0:T(8,128)(2,1)S(1)} %dynamic-slice_bitcast_fusion.15), channel_id=1, source_target_pairs={{0,2},{1,3},{2,0},{3,1},{4,6},{5,7},{6,4},{7,5},{8,10},{9,11},{10,... | collective-permute-start | bytes 393224 | tf_op jit(solution)/shard_map/ppermute | solution.py:30
  539.7 5.2 collective-permute-start.6
  542.5 5.0 collective-permute-start.8
  544.1 5.0 collective-permute-start.17
  549.2 6.0 collective-permute-start.18
  550.8 6.3 collective-permute-start.9
  555.2 4.4 collective-permute-start.19
  557.1 5.2 collective-permute-start.10
  562.4 4.3 collective-permute-start.11
  570.6 14.9 %collective-permute-start.29 = (bf16[4,128,512]{2,1,0:T(8,128)(2,1)S(1)}, bf16[4,128,512]{2,1,0:T(8,128)(2,1)S(1)}, u32[]{:S(2)}, u32[]{:S(2)}) collective-permute-start(bf16[4,128,512]{2,1,0:T(8,128)(2,1)S(1)} %dynamic-slice_bitcast_fusion.1), channel_id=1, source_target_pairs={{0,2},{1,3},{2,0},{3,1},{4,6},{5,7},{6,4},{7,5},{8,10},{9,11},{10,... | collective-permute-start | bytes 1572872 | tf_op jit(solution)/shard_map/ppermute | solution.py:30
  571.0 15.5 %collective-permute-start.31 = (bf16[8,64,512]{2,1,0:T(8,128)(2,1)S(1)}, bf16[8,64,512]{2,1,0:T(8,128)(2,1)S(1)}, u32[]{:S(2)}, u32[]{:S(2)}) collective-permute-start(bf16[8,64,512]{2,1,0:T(8,128)(2,1)S(1)} %dynamic-slice_bitcast_fusion), channel_id=1, source_target_pairs={{0,16},{16,0},{1,17},{17,1},{2,18},{18,2},{3,19},{19,3},{4,20},{20... | collective-permute-start | bytes 1572872 | tf_op jit(solution)/shard_map/ppermute | solution.py:30
  575.1 19.6 %collective-permute-start.21 = (bf16[4,128,512]{2,1,0:T(8,128)(2,1)S(1)}, bf16[4,128,512]{2,1,0:T(8,128)(2,1)S(1)}, u32[]{:S(2)}, u32[]{:S(2)}) collective-permute-start(bf16[4,128,512]{2,1,0:T(8,128)(2,1)S(1)} %dynamic-slice_bitcast_fusion.3), channel_id=1, source_target_pairs={{0,2},{1,3},{2,0},{3,1},{4,6},{5,7},{6,4},{7,5},{8,10},{9,11},{10,... | collective-permute-start | bytes 1572872 | tf_op jit(solution)/shard_map/ppermute | solution.py:30
  576.2 20.2 %collective-permute-start.23 = (bf16[8,64,512]{2,1,0:T(8,128)(2,1)S(1)}, bf16[8,64,512]{2,1,0:T(8,128)(2,1)S(1)}, u32[]{:S(2)}, u32[]{:S(2)}) collective-permute-start(bf16[8,64,512]{2,1,0:T(8,128)(2,1)S(1)} %dynamic-slice_bitcast_fusion.2), channel_id=1, source_target_pairs={{0,16},{16,0},{1,17},{17,1},{2,18},{18,2},{3,19},{19,3},{4,20},{20... | collective-permute-start | bytes 1572872 | tf_op jit(solution)/shard_map/ppermute | solution.py:30
  585.7 13.2 %collective-permute-start.30 = (bf16[4,64,512]{2,1,0:T(8,128)(2,1)S(1)}, bf16[4,64,512]{2,1,0:T(8,128)(2,1)S(1)}, u32[]{:S(2)}, u32[]{:S(2)}) collective-permute-start(bf16[4,64,512]{2,1,0:T(8,128)(2,1)S(1)} %dynamic-slice_bitcast_fusion.6), channel_id=1, source_target_pairs={{0,16},{16,0},{1,17},{17,1},{2,18},{18,2},{3,19},{19,3},{4,20},{20... | collective-permute-start | bytes 786440 | tf_op jit(solution)/shard_map/ppermute | solution.py:30
  586.7 12.2 %collective-permute-start.32 = (bf16[4,64,512]{2,1,0:T(8,128)(2,1)S(1)}, bf16[4,64,512]{2,1,0:T(8,128)(2,1)S(1)}, u32[]{:S(2)}, u32[]{:S(2)}) collective-permute-start(bf16[4,64,512]{2,1,0:T(8,128)(2,1)S(1)} %dynamic-slice_bitcast_fusion.5), channel_id=1, source_target_pairs={{0,2},{1,3},{2,0},{3,1},{4,6},{5,7},{6,4},{7,5},{8,10},{9,11},{10,... | collective-permute-start | bytes 786440 | tf_op jit(solution)/shard_map/ppermute | solution.py:30
  594.9 6.7 %collective-permute-start.22 = (bf16[4,64,512]{2,1,0:T(8,128)(2,1)S(1)}, bf16[4,64,512]{2,1,0:T(8,128)(2,1)S(1)}, u32[]{:S(2)}, u32[]{:S(2)}) collective-permute-start(bf16[4,64,512]{2,1,0:T(8,128)(2,1)S(1)} %dynamic-slice_bitcast_fusion.9), channel_id=1, source_target_pairs={{0,16},{16,0},{1,17},{17,1},{2,18},{18,2},{3,19},{19,3},{4,20},{20... | collective-permute-start | bytes 786440 | tf_op jit(solution)/shard_map/ppermute | solution.py:30
  596.6 6.4 %collective-permute-start.24 = (bf16[4,64,512]{2,1,0:T(8,128)(2,1)S(1)}, bf16[4,64,512]{2,1,0:T(8,128)(2,1)S(1)}, u32[]{:S(2)}, u32[]{:S(2)}) collective-permute-start(bf16[4,64,512]{2,1,0:T(8,128)(2,1)S(1)} %dynamic-slice_bitcast_fusion.8), channel_id=1, source_target_pairs={{0,2},{1,3},{2,0},{3,1},{4,6},{5,7},{6,4},{7,5},{8,10},{9,11},{10,... | collective-permute-start | bytes 786440 | tf_op jit(solution)/shard_map/ppermute | solution.py:30
  599.1 6.4 %collective-permute-start.33 = (bf16[2,128,512]{2,1,0:T(8,128)(2,1)S(1)}, bf16[2,128,512]{2,1,0:T(8,128)(2,1)S(1)}, u32[]{:S(2)}, u32[]{:S(2)}) collective-permute-start(bf16[2,128,512]{2,1,0:T(8,128)(2,1)S(1)} %dynamic-slice_bitcast_fusion.4), channel_id=1, source_target_pairs={{0,4},{1,5},{2,6},{3,7},{4,0},{5,1},{6,2},{7,3},{8,12},{9,13},{10,... | collective-permute-start | bytes 786440 | tf_op jit(solution)/shard_map/ppermute | solution.py:30
  605.6 7.4 %collective-permute-start.34 = (bf16[1,128,512]{2,1,0:T(8,128)(2,1)S(1)}, bf16[1,128,512]{2,1,0:T(8,128)(2,1)S(1)}, u32[]{:S(2)}, u32[]{:S(2)}) collective-permute-start(bf16[1,128,512]{2,1,0:T(8,128)(2,1)S(1)} %constant_dynamic-slice_fusion.8), channel_id=1, source_target_pairs={{0,8},{1,9},{2,10},{3,11},{4,12},{5,13},{6,14},{7,15},{8,0},{9,1},... | collective-permute-start | bytes 393224 | tf_op jit(solution)/shard_map/ppermute | solution.py:30
  606.6 8.0 %collective-permute-start.25 = (bf16[2,128,512]{2,1,0:T(8,128)(2,1)S(1)}, bf16[2,128,512]{2,1,0:T(8,128)(2,1)S(1)}, u32[]{:S(2)}, u32[]{:S(2)}) collective-permute-start(bf16[2,128,512]{2,1,0:T(8,128)(2,1)S(1)} %dynamic-slice_bitcast_fusion.7), channel_id=1, source_target_pairs={{0,4},{1,5},{2,6},{3,7},{4,0},{5,1},{6,2},{7,3},{8,12},{9,13},{10,... | collective-permute-start | bytes 786440 | tf_op jit(solution)/shard_map/ppermute | solution.py:30
  613.1 5.0 collective-permute-start.35
  614.7 7.2 %collective-permute-start.26 = (bf16[1,128,512]{2,1,0:T(8,128)(2,1)S(1)}, bf16[1,128,512]{2,1,0:T(8,128)(2,1)S(1)}, u32[]{:S(2)}, u32[]{:S(2)}) collective-permute-start(bf16[1,128,512]{2,1,0:T(8,128)(2,1)S(1)} %constant_dynamic-slice_fusion.9), channel_id=1, source_target_pairs={{0,8},{1,9},{2,10},{3,11},{4,12},{5,13},{6,14},{7,15},{8,0},{9,1},... | collective-permute-start | bytes 393224 | tf_op jit(solution)/shard_map/ppermute | solution.py:30
  621.9 5.0 collective-permute-start.27
  (72 other events, 465.5 us)
Sparse Core Ops, SparseCore 0:
  10.8 44.3 all-gather.11
  58.0 40.3 all-gather.15
  101.2 40.0 all-gather.17
  143.3 40.1 all-gather.13
  185.5 40.1 all-gather.19
  227.7 40.1 all-gather.21
  393.8 118.2 all-reduce.13
